TPU v7x, 256 devices: a whole 4x4x8 slice. The times are simulated.
256 devices in a mesh: ctx: 32 (over z_lo, x, y), tp: 8 (over z_hi, core).
Axes of the slice: x: 4, y: 4, z: 8 (z_hi: 4, z_lo: 2; z = z_hi * 2 + z_lo), core: 2. Of those that a mesh axis runs over, the one named last changes fastest.
Arguments:
- queries: bfloat16 [4096, 8192], P('ctx', 'tp'), may hold values from -8 to 8
- span_kv: bfloat16 [4096, 8, 2, 128], P('ctx', 'tp'), may hold values from -8 to 8
- cache_kv: bfloat16 [16384, 8, 2, 128], P('ctx', 'tp'), may hold values from -4 to 4
- out_weight: bfloat16 [8192, 8192], P('tp', 'ctx'), may hold values from -2.390625 to 2.390625
- offset: int32 [1], replicated, may hold values from 16384 to 24575
- lengths: int32 [64], replicated, may hold values from 64 to 256, as said below
Outputs:
- mixed: bfloat16 [4096, 8192], P('tp', 'ctx')
Inputs may be any that keep to these rules, and one draw needn't show every extreme that they name: `lengths`: each at most 256; in every draw some match has all 256 of its positions valid.
All inputs are finite; a program needn't handle non-finite values.
Results may differ from a plain program's by a relative error of at most 0.025.
Values may be sent and summed in bfloat16 or wider, within the bound.
A program may use at most 64 MiB of HBM per device.

v0:
```python
import math

import jax
import jax.numpy as jnp
from jax import lax
from jax.sharding import PartitionSpec as P

SLOT = 256


lowest_score = -1e30
rope_base = 500000.0


def rotate(values, positions):
    head_size = values.shape[-1]
    half_dim = head_size // 2
    frequency = jnp.exp(
        jnp.arange(half_dim, dtype=jnp.float32) * (-2.0 * math.log(rope_base) / head_size)
    )
    angles = positions.astype(jnp.float32)[:, None] * frequency[None, :]
    cosine = jnp.cos(angles)[:, None, :]
    sine_part = jnp.sin(angles)[:, None, :]
    first_half = values[..., :half_dim]
    second_half = values[..., half_dim:]
    return jnp.concatenate(
        [
            first_half * cosine - second_half * sine_part,
            second_half * cosine + first_half * sine_part,
        ],
        axis=-1,
    )


def key_block(count):
    for option in (2048, 1536, 1024, 768, 512, 384, 256, 128):
        return option
    return count


def slot_valid(cache_positions, lengths):
    match_ids = jnp.arange(lengths.shape[0], dtype=jnp.int32)
    owner = cache_positions // SLOT
    limit = jnp.sum(jnp.where(owner[:, None] == match_ids[None, :], lengths[None, :], 0), axis=1)
    return cache_positions % SLOT < limit


def online_update(carry_state, grouped, key_rows, value_rows, valid, scale):
    running_max, running_sum, accum = carry_state
    scores = (
        jnp.einsum("tkgd,nkd->tkgn", grouped, key_rows, preferred_element_type=jnp.float32) * scale
    )
    scores = jnp.where(valid, scores, lowest_score)
    new_max = jnp.maximum(running_max, jnp.max(scores, axis=-1))
    factor = jnp.exp(running_max - new_max)
    weights = jnp.where(valid, jnp.exp(scores - new_max[..., None]), 0.0)
    running_sum = running_sum * factor + jnp.sum(weights, axis=-1)
    update = jnp.einsum(
        "tkgn,nkd->tkgd",
        weights.astype(jnp.bfloat16),
        value_rows,
        preferred_element_type=jnp.float32,
    )
    accum = accum * factor[..., None] + update
    return (new_max, running_sum, accum)


def fold_blocks(carry_state, grouped, piece, mask_rule, scale):
    count = piece.shape[0]
    block = key_block(count)
    block_count = count // block
    kv_local = piece.shape[1]
    head_size = piece.shape[3]
    key_rows = piece[:, :, 0, :].reshape(block_count, block, kv_local, head_size)
    value_rows = piece[:, :, 1, :].reshape(block_count, block, kv_local, head_size)

    def advance(state_now, inputs):
        block_keys, block_values, index = inputs
        positions = index * block + jnp.arange(block, dtype=jnp.int32)
        valid = mask_rule(positions)
        return (online_update(state_now, grouped, block_keys, block_values, valid, scale), None)

    result, unused = lax.scan(
        advance, carry_state, (key_rows, value_rows, jnp.arange(block_count, dtype=jnp.int32))
    )
    return result


def body(queries, span_kv, cache_kv, out_weight, offset, lengths):
    tok_rows, width = queries.shape
    kv_local = span_kv.shape[1]
    head_size = span_kv.shape[3]
    heads_local = width // head_size
    group = heads_local // kv_local
    scale = 1.0 / math.sqrt(head_size)
    ctx_index = lax.axis_index("ctx")
    first_token = ctx_index * tok_rows
    token_ids = first_token + jnp.arange(tok_rows, dtype=jnp.int32)
    positions = offset[0] + token_ids
    rotated = rotate(
        queries.reshape(tok_rows, heads_local, head_size).astype(jnp.float32), positions
    ).astype(jnp.bfloat16)
    grouped = rotated.reshape(tok_rows, kv_local, group, head_size)
    span_keys = rotate(span_kv[:, :, 0, :].astype(jnp.float32), positions).astype(jnp.bfloat16)
    span_rotated = jnp.stack([span_keys, span_kv[:, :, 1, :]], axis=2)

    def cache_rule(key_positions):
        return slot_valid(key_positions, lengths)[None, None, None, :]

    def span_rule(key_positions):
        return (key_positions[None, :] <= token_ids[:, None])[:, None, None, :]

    start_state = (
        jnp.full((tok_rows, kv_local, group), lowest_score, jnp.float32),
        jnp.zeros((tok_rows, kv_local, group), jnp.float32),
        jnp.zeros((tok_rows, kv_local, group, head_size), jnp.float32),
    )
    state_now = fold_blocks(
        start_state, grouped, lax.all_gather(cache_kv, "ctx", axis=0, tiled=True), cache_rule, scale
    )
    state_now = fold_blocks(
        state_now,
        grouped,
        lax.all_gather(span_rotated, "ctx", axis=0, tiled=True),
        span_rule,
        scale,
    )
    attention = (state_now[2] / state_now[1][..., None]).astype(jnp.bfloat16)
    attention = attention.reshape(tok_rows, heads_local * head_size)
    projected = jnp.dot(
        lax.all_gather(attention, "ctx", axis=0, tiled=True),
        out_weight,
        preferred_element_type=jnp.float32,
    )
    return lax.psum_scatter(projected.astype(jnp.bfloat16), "tp", scatter_dimension=0, tiled=True)


def solution(mesh):
    return jax.shard_map(
        body,
        mesh=mesh,
        in_specs=(
            P("ctx", "tp"),
            P("ctx", "tp", None, None),
            P("ctx", "tp", None, None),
            P("tp", "ctx"),
            P(),
            P(),
        ),
        out_specs=P("tp", "ctx"),
        check_vma=False,
    )
```

profile of v0, /device:TPU:1, one launch (start us, length us, event | category | flops | bytes accessed | tf_op | source)
XLA Modules:
  0.0 689.4 jit_solution(2015191303401559980)
XLA Ops:
  7.3 1.0 fusion.74
  9.5 1.7 copy.27
  11.3 1.1 copy.28
  12.9 112.2 %all-gather.6.cloned.1.call-done = bf16[4096,1,2,128]{0,3,2,1:T(8,128)(2,1)} async-done(((bf16[128,1,2,128]{0,3,2,1:T(8,128)(2,1)}), bf16[4096,1,2,128]{0,3,2,1:T(8,128)(2,1)}) %all-gather.6.cloned.1.call-update) | async-done | bytes 2097168 | tf_op jit(solution)/shard_map/all_gather | solution.py:124
  125.1 2.7 fusion.73
  127.9 1.6 copy.34
  129.5 1.3 copy.35
  130.8 162.1 %all-gather.4.cloned.1.call-done = bf16[16384,1,2,128]{3,0,2,1:T(8,128)(2,1)} async-done(((bf16[512,1,2,128]{3,0,2,1:T(8,128)(2,1)}), bf16[16384,1,2,128]{3,0,2,1:T(8,128)(2,1)}) %all-gather.4.cloned.1.call-update) | async-done | bytes 8388624 | tf_op jit(solution)/shard_map/all_gather | solution.py:119
  292.9 5.7 fusion.72
  298.6 126.6 %while.33 = (s32[]{:T(128)}, f32[128,1,8]{0,2,1:T(8,128)S(1)}, f32[128,1,8]{0,2,1:T(8,128)S(1)}, f32[128,1,8,128]{0,3,2,1:T(8,128)S(1)}, s32[8]{0:T(128)S(1)}, /...) while((s32[]{:T(128)}, f32[128,1,8]{0,2,1:T(8,128)S(1)}, ...), condition=%wide.region_4.5_spmd.clone, body=%wide.region_0.4_spmd.clone.sunk | while | flops 1101854720 | bytes 52800976 | solution.py:83
  300.0 5.6 bitcast_reduce_fusion.2
  305.6 5.2 fusion.100
  311.7 2.7 fusion.99
  315.9 5.6 bitcast_reduce_fusion.2
  321.5 5.2 fusion.100
  326.7 0.8 slice-done.1
  327.5 2.7 fusion.99
  331.7 5.6 bitcast_reduce_fusion.2
  337.3 5.2 fusion.100
  343.4 2.7 fusion.99
  347.5 5.6 bitcast_reduce_fusion.2
  353.1 5.2 fusion.100
  358.4 0.8 slice-done.1
  359.2 2.7 fusion.99
  363.3 5.6 bitcast_reduce_fusion.2
  368.9 5.2 fusion.100
  375.0 2.7 fusion.99
  379.2 5.6 bitcast_reduce_fusion.2
  384.8 5.2 fusion.100
  390.0 0.8 slice-done.1
  390.8 2.7 fusion.99
  395.0 5.6 bitcast_reduce_fusion.2
  400.6 5.2 fusion.100
  406.7 2.7 fusion.99
  410.8 5.6 bitcast_reduce_fusion.2
  416.4 5.2 fusion.100
  421.7 0.8 slice-done.1
  422.5 2.7 fusion.99
  425.2 14.6 %while.32 = (s32[]{:T(128)}, f32[128,1,8]{0,2,1:T(8,128)S(1)}, f32[128,1,8]{0,2,1:T(8,128)S(1)}, f32[128,1,8,128]{0,3,2,1:T(8,128)S(1)}, s32[2]{0:T(128)S(1)}, /...) while((s32[]{:T(128)}, f32[128,1,8]{0,2,1:T(8,128)S(1)}, ...), condition=%wide.region_8.9_spmd.clone, body=%wide.region_5.8_spmd.clone.sunk | while | flops 1101534336 | bytes 32851120 | solution.py:83
  426.8 1.4 fusion.91
  428.2 2.2 fusion.94
  430.4 2.0 fusion.93
  434.1 1.4 fusion.91
  435.5 2.2 fusion.94
  437.7 2.0 fusion.93
  440.8 173.2 %all-gather.8.cloned.1.call-done = bf16[4096,1024]{0,1:T(8,128)(2,1)} async-done(((bf16[128,1024]{0,1:T(8,128)(2,1)}), bf16[4096,1024]{0,1:T(8,128)(2,1)}) %all-gather.8.cloned.1.call-update) | async-done | bytes 8388624 | tf_op jit(solution)/shard_map/all_gather | solution.py:131
  614.0 7.2 %convolution_convert_fusion = bf16[4096,256]{1,0:T(8,128)(2,1)} fusion(bf16[4096,1024]{0,1:T(8,128)(2,1)} %all-gather.8.cloned.1.call-done, bf16[1024,256]{1,0:T(8,128)(2,1)S(1)} %copy-done), kind=kOutput, calls=%fused_computation.74 | convolution fusion | flops 2148532224 | bytes 11010048 | tf_op jit(solution)/shard_map/dot_general | solution.py:130
  621.3 61.6 %reduce-scatter.2.cloned.1.call-done = bf16[512,256]{1,0:T(8,128)(2,1)} async-done(((bf16[4096,256]{1,0:T(8,128)(2,1)}), bf16[512,256]{1,0:T(8,128)(2,1)}) %reduce-scatter.2.cloned.1.call-update) | async-done | bytes 262160 | tf_op jit(solution)/shard_map/reduce_scatter | solution.py:135
  (140 shorter events, 14.3 us)
Async XLA Ops:
  6.5 607.5 %copy-start = (bf16[1024,256]{1,0:T(8,128)(2,1)S(1)}, bf16[1024,256]{1,0:T(8,128)(2,1)}, u32[]{:S(2)}) copy-start(bf16[1024,256]{1,0:T(8,128)(2,1)} %param.13) | copy-start | bytes 1572868
  6.5 118.6 %all-gather.6.cloned.1.call-start = ((), (), s32[]{:S(2)}) async-start(), calls=%async_computation.2 | async-start | bytes 2162688 | tf_op jit(solution)/shard_map/all_gather | solution.py:124
  9.4 283.4 %all-gather.4.cloned.1.call-start = ((), (), s32[]{:S(2)}) async-start(), calls=%async_computation.1 | async-start | bytes 8650752 | tf_op jit(solution)/shard_map/all_gather | solution.py:119
  11.2 602.8 %all-gather.8.cloned.1.call-start = ((), (), s32[]{:S(2)}) async-start(), calls=%async_computation.3 | async-start | bytes 8650752 | tf_op jit(solution)/shard_map/all_gather | solution.py:131
  130.8 167.8 %copy-start.2 = (s32[64]{0:T(128)S(1)}, s32[64]{0:T(128)}, u32[]{:S(2)}) copy-start(s32[64]{0:T(128)} %param.15) | copy-start | bytes 772
  305.6 5.3 slice-start
  305.6 6.1 slice-start.1
  321.4 5.3 slice-start
  321.5 6.1 slice-start.1
  337.3 5.3 slice-start
  337.3 6.1 slice-start.1
  353.1 5.3 slice-start
  353.1 6.1 slice-start.1
  368.9 5.3 slice-start
  368.9 6.1 slice-start.1
  384.8 5.3 slice-start
  384.8 6.1 slice-start.1
  400.6 5.3 slice-start
  400.6 6.1 slice-start.1
  416.4 5.3 slice-start
  416.4 6.1 slice-start.1
  425.2 3.0 copy-start.1
  432.5 3.0 copy-start.1
  440.6 242.4 %reduce-scatter.2.cloned.1.call-start = ((), (), s32[]{:S(2)}) async-start(), calls=%async_computation.4 | async-start | bytes 2359296 | tf_op jit(solution)/shard_map/reduce_scatter | solution.py:135
Sparse Core Ops, SparseCore 0:
  9.6 115.5 all-gather.5
  126.9 165.8 all-gather.3
  440.7 173.3 all-gather.7
  621.4 61.4 reduce-scatter.1
where the time goes:
time: 691 us; the launch traced here: 689 us
  waiting for transfers between devices  509 us (74%)
  matrix products  101 us (15%)
  other arithmetic  29.7 us (4%)
  local copies, waits for them, and re-layouts  28 us (4%)
  between operations  14 us (2%)
  loops' own time  7.33 us (1%)
    all_gather x1, waiting for transfers between devices, body(): lax.all_gather(attention, 'ctx', axis=0, tiled=True)  173 us
    all_gather x1, waiting for transfers between devices, body(): lax.all_gather(cache_kv, 'ctx', axis=0, tiled=True)  162 us
    all_gather x1, waiting for transfers between devices, body(): lax.all_gather(span_rotated, 'ctx', axis=0, tiled=True)  112 us
    reduce_scatter x1, waiting for transfers between devices, body(): lax.psum_scatter(projected.astype(jnp.bfloat16), 'tp', scatter_dimension=...  61.6 us
    dot_general x10, matrix products, online_update(): jnp.einsum('tkgd,nkd->tkgn', grouped, key_rows, preferred_element_type=jn...  47.4 us
    dot_general x10, matrix products, online_update(): jnp.einsum('tkgn,nkd->tkgd', weights.astype(jnp.bfloat16), value_rows, pr...  46.3 us
    reduce_sum x10, other arithmetic, online_update(): running_sum = running_sum * factor + jnp.sum(weights, axis=-1)  25.3 us
  transfers between devices with their start and end apart: 4, of which 4 were waited for; matrix products, arithmetic and copies ran while one was open for 1% of the time, Pallas kernels for 0%

commit v1 on v0

v1 whole, which is shorter than its diff:
```python
import math

import jax
import jax.numpy as jnp
from jax import lax
from jax.experimental import pallas as pl
from jax.experimental.pallas import tpu as pltpu
from jax.sharding import PartitionSpec as P

SLOT = 256
HD = 128
TOK = 128
HEADS = 8
KV_ROWS = 640
CACHE_ROWS = 512
CH = 512
NCH = 10
A_ROWS = 256
lowest_score = -1e30
rope_base = 500000.0
MESH = pl.DeviceIdType.MESH
SCALE2 = math.log2(math.e) / math.sqrt(HD)


def rotate(values, positions):
    head_size = values.shape[-1]
    half_dim = head_size // 2
    frequency = jnp.exp(
        jnp.arange(half_dim, dtype=jnp.float32) * (-2.0 * math.log(rope_base) / head_size)
    )
    angles = positions.astype(jnp.float32)[:, None] * frequency[None, :]
    cosine = jnp.cos(angles)[:, None, :]
    sine_part = jnp.sin(angles)[:, None, :]
    first_half = values[..., :half_dim]
    second_half = values[..., half_dim:]
    return jnp.concatenate(
        [
            first_half * cosine - second_half * sine_part,
            second_half * cosine + first_half * sine_part,
        ],
        axis=-1,
    )


def coords():
    c = lax.axis_index("ctx")
    z = c // 16
    x = (c // 4) % 4
    y = c % 4
    return z, x, y


def ctx_of(z, x, y):
    return z * 16 + x * 4 + y


def entry_barrier(devices):
    barrier = pltpu.get_barrier_semaphore()
    for d in devices:
        pl.semaphore_signal(barrier, inc=1, device_id=d, device_id_type=MESH)
    pl.semaphore_wait(barrier, len(devices))


class Sender:
    def __init__(self, ssem, rsem):
        self.ssem, self.rsem, self.count, self.sent = ssem, rsem, 0, []

    def __call__(self, src, dst, device):
        n = self.count
        self.count += 1
        copy = pltpu.make_async_remote_copy(
            src_ref=src,
            dst_ref=dst,
            send_sem=self.ssem.at[n],
            recv_sem=self.rsem.at[n],
            device_id=device,
            device_id_type=MESH,
        )
        copy.start()
        self.sent.append(copy)
        return copy

    def finish(self):
        for copy in self.sent:
            copy.wait_send()


GATHER_COPIES = 22


def gather_kernel(q_ref, kv_ref, q4_ref, kvg_ref, ssem, rsem, lsem):
    z, x, y = coords()
    xp, xm, x2 = (x + 1) % 4, (x + 3) % 4, (x + 2) % 4
    yp, ym = (y + 1) % 4, (y + 3) % 4
    zo = 1 - z
    dz = {"ctx": ctx_of(zo, x, y)}
    dxp = {"ctx": ctx_of(z, xp, y)}
    dxm = {"ctx": ctx_of(z, xm, y)}
    dyp = {"ctx": ctx_of(z, x, yp)}
    dym = {"ctx": ctx_of(z, x, ym)}
    a = pl.ds(0, A_ROWS)
    a0 = pl.ds(0, A_ROWS // 2)
    a1 = pl.ds(A_ROWS // 2, A_ROWS // 2)
    nb = KV_ROWS - A_ROWS
    b = pl.ds(A_ROWS, nb)
    b0 = pl.ds(A_ROWS, nb // 2)
    b1 = pl.ds(A_ROWS + nb // 2, nb // 2)
    t0 = pl.ds(0, TOK // 2)
    t1 = pl.ds(TOK // 2, TOK // 2)

    own = z * 4 + x
    lq = pltpu.make_async_copy(q_ref, q4_ref.at[y], lsem.at[0])
    lkv = pltpu.make_async_copy(kv_ref, kvg_ref.at[own], lsem.at[1])
    entry_barrier([dz, dxp, dxm, dyp, dym])
    lq.start()
    lkv.start()
    send = Sender(ssem, rsem)

    def kv(j, rows):
        return kvg_ref.at[j, rows]

    def pass_on(j, rows, device):
        return send(kv(j, rows), kv(j, rows), device)

    b_z = send(kv_ref.at[b], kv(own, b), dz)
    b_xp = send(kv_ref.at[b], kv(own, b), dxp)
    b_xm = send(kv_ref.at[b], kv(own, b), dxm)
    q_yp = send(q_ref, q4_ref.at[y], dyp)
    q_ym = send(q_ref, q4_ref.at[y], dym)
    a_xp = send(kv_ref.at[a], kv(own, a), dxp)
    a_xm = send(kv_ref.at[a], kv(own, a), dxm)
    a_z = send(kv_ref.at[a], kv(own, a), dz)
    b_z.wait_recv()
    oz = zo * 4 + x
    bz_xp = pass_on(oz, b, dxp)
    bz_xm = pass_on(oz, b, dxm)
    b_xp.wait_recv()
    bf_xp = pass_on(z * 4 + xm, b0, dxp)
    b_xm.wait_recv()
    bf_xm = pass_on(z * 4 + xp, b1, dxm)
    q_yp.wait_recv()
    qf_yp = send(q4_ref.at[ym, t0], q4_ref.at[ym, t0], dyp)
    q_ym.wait_recv()
    qf_ym = send(q4_ref.at[yp, t1], q4_ref.at[yp, t1], dym)
    a_xp.wait_recv()
    af_xp = pass_on(z * 4 + xm, a0, dxp)
    az_m = pass_on(z * 4 + xm, a, dz)
    a_xm.wait_recv()
    af_xm = pass_on(z * 4 + xp, a1, dxm)
    az_p = pass_on(z * 4 + xp, a, dz)
    bz_xp.wait_recv()
    bzf_xp = pass_on(zo * 4 + xm, b0, dxp)
    bz_xm.wait_recv()
    bzf_xm = pass_on(zo * 4 + xp, b1, dxm)
    af_xp.wait_recv()
    az_2a = pass_on(z * 4 + x2, a0, dz)
    af_xm.wait_recv()
    az_2b = pass_on(z * 4 + x2, a1, dz)
    for copy in (a_z, bf_xp, bf_xm, qf_yp, qf_ym, az_m, az_p, bzf_xp, bzf_xm, az_2a, az_2b):
        copy.wait_recv()
    send.finish()
    lq.wait()
    lkv.wait()


def gather(q, kv):
    return pl.pallas_call(
        gather_kernel,
        name="gather_qkv",
        out_shape=(
            jax.ShapeDtypeStruct((4, TOK, HEADS * HD), jnp.bfloat16),
            jax.ShapeDtypeStruct((8, KV_ROWS, 2 * HD), jnp.bfloat16),
        ),
        in_specs=[pl.BlockSpec(memory_space=pltpu.VMEM)] * 2,
        out_specs=[pl.BlockSpec(memory_space=pltpu.VMEM)] * 2,
        scratch_shapes=[
            pltpu.SemaphoreType.DMA((GATHER_COPIES,)),
            pltpu.SemaphoreType.DMA((GATHER_COPIES,)),
            pltpu.SemaphoreType.DMA((2,)),
        ],
        compiler_params=pltpu.CompilerParams(
            collective_id=0, has_side_effects=True, vmem_limit_bytes=16 << 20
        ),
    )(q, kv)


ROWS = HEADS * TOK


def attention_kernel(
    lens_ref, q4_ref, kvg_ref, o4_ref, st_ref, qh, kbuf, vbuf, bias, sbuf, sown, mx, mc, lsum, acc
):
    z, x, y = coords()
    j0 = z * 4 + x
    for yy in range(4):
        for h in range(HEADS):
            qh[yy, h * TOK : (h + 1) * TOK, :] = q4_ref[yy, :, h * HD : (h + 1) * HD]

    pos = lax.broadcasted_iota(jnp.int32, bias.shape, 0) * CH + lax.broadcasted_iota(
        jnp.int32, bias.shape, 1
    )
    mask = jnp.full(bias.shape, lowest_score, jnp.float32)
    off = jnp.int32(0)
    for j in range(8):
        for s in range(2):
            n = lens_ref[2 * (4 * j + y) + s]
            o = pl.multiple_of(off, 16)
            rows = pl.ds(s * SLOT, SLOT)
            kbuf[pl.ds(o, SLOT), :] = kvg_ref[j, rows, 0:HD]
            vbuf[pl.ds(o, SLOT), :] = kvg_ref[j, rows, HD : 2 * HD]
            mask = jnp.where((pos >= off) & (pos < off + n), 0.0, mask)
            off = off + ((n + 15) // 16) * 16
    for j in range(7):
        o = pl.multiple_of(off + j * TOK, 16)
        rows = pl.ds(CACHE_ROWS, TOK)
        kbuf[pl.ds(o, TOK), :] = kvg_ref[j, rows, 0:HD]
        vbuf[pl.ds(o, TOK), :] = kvg_ref[j, rows, HD : 2 * HD]
    total = off + j0 * TOK
    mask = jnp.where((pos >= off) & (pos < total), 0.0, mask)
    bias[...] = mask
    o = pl.multiple_of(total, 16)
    kbuf[pl.ds(o, CH), :] = jnp.zeros((CH, HD), jnp.bfloat16)
    vbuf[pl.ds(o, CH), :] = jnp.zeros((CH, HD), jnp.bfloat16)
    chunks = (total + CH - 1) // CH

    row_tok = lax.broadcasted_iota(jnp.int32, (TOK, TOK), 0)
    key_tok = lax.broadcasted_iota(jnp.int32, (TOK, TOK), 1)

    def scores(rows, keys):
        return lax.dot_general(
            rows, keys, (((1,), (1,)), ((), ())), preferred_element_type=jnp.float32
        )

    def fold(op, values):
        out = values[:, 0:HD]
        for n in range(1, values.shape[1] // HD):
            out = op(out, values[:, n * HD : (n + 1) * HD])
        return out

    def first_own(i, slot):
        own_keys = kvg_ref[j0, CACHE_ROWS:KV_ROWS, 0:HD]
        s = scores(qh[i], own_keys)
        ok = (key_tok + (y - i) * TOK) <= row_tok
        own_bias = jnp.where(ok, 0.0, lowest_score)
        s = s + jnp.concatenate([own_bias] * HEADS, axis=0)
        sown[slot] = s
        mx[...] = s

    def first_step(kc, i, slot):
        k0 = pl.multiple_of(kc * CH, CH)
        s = scores(qh[i], kbuf[pl.ds(k0, CH), :]) + bias[pl.ds(kc, 1), :]
        sbuf[slot, kc] = s
        mx[...] = jnp.maximum(mx[...], fold(jnp.maximum, s))

    def first_end():
        m = jnp.max(mx[...], axis=1, keepdims=True)
        mc[...] = jnp.broadcast_to(m * SCALE2, (ROWS, HD))

    def second_own(slot):
        own_values = kvg_ref[j0, CACHE_ROWS:KV_ROWS, HD : 2 * HD]
        p = jnp.exp2(sown[slot] * SCALE2 - mc[...])
        lsum[...] = p
        acc[...] = jnp.dot(p.astype(jnp.bfloat16), own_values, preferred_element_type=jnp.float32)

    def second_step(kc, slot):
        k0 = pl.multiple_of(kc * CH, CH)
        m = mc[...]
        p = jnp.exp2(sbuf[slot, kc] * SCALE2 - jnp.concatenate([m] * (CH // HD), axis=1))
        lsum[...] += fold(jnp.add, p)
        acc[...] += jnp.dot(
            p.astype(jnp.bfloat16), vbuf[pl.ds(k0, CH), :], preferred_element_type=jnp.float32
        )

    def second_end(i):
        l = jnp.broadcast_to(jnp.sum(lsum[...], axis=1, keepdims=True), (ROWS, HD))
        o = acc[...] / l
        lse = mc[...] + jnp.log2(l)
        lane = lax.broadcasted_iota(jnp.int32, (TOK, HD), 1)
        packed = jnp.zeros((TOK, HD), jnp.float32)
        for h in range(HEADS):
            rows = slice(h * TOK, (h + 1) * TOK)
            o4_ref[i, :, h * HD : (h + 1) * HD] = o[rows].astype(jnp.bfloat16)
            packed = jnp.where(lane == h, lse[rows], packed)
        st_ref[i] = packed.T[0:HEADS]

    first_own(0, 0)

    @pl.loop(0, chunks)
    def _(kc):
        first_step(kc, 0, 0)

    first_end()

    for i in range(4):
        slot = i % 2
        second_own(slot)
        if i < 3:
            first_own(i + 1, 1 - slot)

        @pl.loop(0, chunks)
        def _(kc, i=i, slot=slot):
            if i < 3:
                first_step(kc, i + 1, 1 - slot)
            second_step(kc, slot)

        second_end(i)
        if i < 3:
            first_end()


def attention(lengths, q4, kvg):
    rows = NCH * CH + CH
    return pl.pallas_call(
        attention_kernel,
        name="attention",
        out_shape=(
            jax.ShapeDtypeStruct((4, TOK, HEADS * HD), jnp.bfloat16),
            jax.ShapeDtypeStruct((4, HEADS, TOK), jnp.float32),
        ),
        in_specs=[
            pl.BlockSpec(memory_space=pltpu.SMEM),
            pl.BlockSpec(memory_space=pltpu.VMEM),
            pl.BlockSpec(memory_space=pltpu.VMEM),
        ],
        out_specs=[pl.BlockSpec(memory_space=pltpu.VMEM)] * 2,
        scratch_shapes=[
            pltpu.VMEM((4, ROWS, HD), jnp.bfloat16),
            pltpu.VMEM((rows, HD), jnp.bfloat16),
            pltpu.VMEM((rows, HD), jnp.bfloat16),
            pltpu.VMEM((16, CH), jnp.float32),
            pltpu.VMEM((2, NCH, ROWS, CH), jnp.float32),
            pltpu.VMEM((2, ROWS, HD), jnp.float32),
            pltpu.VMEM((ROWS, HD), jnp.float32),
            pltpu.VMEM((ROWS, HD), jnp.float32),
            pltpu.VMEM((ROWS, HD), jnp.float32),
            pltpu.VMEM((ROWS, HD), jnp.float32),
        ],
        compiler_params=pltpu.CompilerParams(vmem_limit_bytes=62 << 20),
    )(lengths, q4, kvg)


COMBINE_COPIES = 8
PLANE_COPIES = 40


def combine_kernel(
    o4_ref, st_ref, w_ref, att_ref, wz_ref, part, stat, fwd, mine, ssem, rsem, ssem2, rsem2, lsem
):
    z, x, y = coords()
    xp, xm, x2 = (x + 1) % 4, (x + 3) % 4, (x + 2) % 4
    yp, ym, y2 = (y + 1) % 4, (y + 3) % 4, (y + 2) % 4
    dz = {"ctx": ctx_of(1 - z, x, y)}
    dxp = {"ctx": ctx_of(z, xp, y)}
    dxm = {"ctx": ctx_of(z, xm, y)}
    dyp = {"ctx": ctx_of(z, x, yp)}
    dym = {"ctx": ctx_of(z, x, ym)}
    dy2 = {"ctx": ctx_of(z, x, y2)}
    half = TOK // 2
    t0 = pl.ds(0, half)
    t1 = pl.ds(half, half)
    entry_barrier([dz, dxp, dxm, dyp, dym, dy2])
    send = Sender(ssem, rsem)
    far_p = send(o4_ref.at[y2, t0], fwd.at[0], dyp)
    far_m = send(o4_ref.at[y2, t1], fwd.at[1], dym)
    to_p = send(o4_ref.at[yp], part.at[2], dyp)
    to_m = send(o4_ref.at[ym], part.at[0], dym)
    st_p = send(st_ref.at[yp], stat.at[2], dyp)
    st_m = send(st_ref.at[ym], stat.at[0], dym)
    st_2 = send(st_ref.at[y2], stat.at[1], dy2)
    swap = send(w_ref, wz_ref, dz)
    send2 = Sender(ssem2, rsem2)
    far_p.wait_recv()
    fw_p = send2(fwd.at[0], part.at[1, t0], dyp)
    far_m.wait_recv()
    fw_m = send2(fwd.at[1], part.at[1, t1], dym)
    for copy in (st_p, st_m, st_2):
        copy.wait_recv()
    s_own = st_ref[y]
    s_p, s_m, s_2 = stat[0], stat[2], stat[1]
    top = jnp.maximum(jnp.maximum(s_own, s_p), jnp.maximum(s_m, s_2))
    e_own = jnp.exp2(s_own - top)
    e_p = jnp.exp2(s_p - top)
    e_m = jnp.exp2(s_m - top)
    e_2 = jnp.exp2(s_2 - top)
    norm = 1.0 / (e_own + e_p + e_m + e_2)
    table = jnp.concatenate(
        [e_own * norm, e_p * norm, e_m * norm, e_2 * norm, jnp.zeros((96, TOK), jnp.float32)],
        axis=0,
    ).T
    for copy in (to_p, to_m, fw_p, fw_m):
        copy.wait_recv()
    for h in range(HEADS):
        lanes = slice(h * HD, (h + 1) * HD)
        out = o4_ref[y, :, lanes].astype(jnp.float32) * table[:, h : h + 1]
        out += part[0, :, lanes].astype(jnp.float32) * table[:, 8 + h : 9 + h]
        out += part[2, :, lanes].astype(jnp.float32) * table[:, 16 + h : 17 + h]
        out += part[1, :, lanes].astype(jnp.float32) * table[:, 24 + h : 25 + h]
        mine[:, lanes] = out.astype(jnp.bfloat16)

    own = x * 4 + y
    local = pltpu.make_async_copy(mine, att_ref.at[own], lsem.at[0])
    local.start()

    quarter = half // 2
    a, a0, a1 = t0, pl.ds(0, quarter), pl.ds(quarter, quarter)
    b, b0, b1 = t1, pl.ds(half, quarter), pl.ds(half + quarter, quarter)

    def pass_on(slot, rows, device):
        return send2(att_ref.at[slot, rows], att_ref.at[slot, rows], device)

    ax_p = send2(mine.at[a], att_ref.at[own, a], dxp)
    ax_m = send2(mine.at[a], att_ref.at[own, a], dxm)
    by_p = send2(mine.at[b], att_ref.at[own, b], dyp)
    by_m = send2(mine.at[b], att_ref.at[own, b], dym)
    ay = {}
    bx = {}
    ay[0] = (
        send2(mine.at[a], att_ref.at[own, a], dyp),
        send2(mine.at[a], att_ref.at[own, a], dym),
    )
    bx[0] = (
        send2(mine.at[b], att_ref.at[own, b], dxp),
        send2(mine.at[b], att_ref.at[own, b], dxm),
    )
    ax_p.wait_recv()
    axf_p = pass_on(xm * 4 + y, a0, dxp)
    by_p.wait_recv()
    byf_p = pass_on(x * 4 + ym, b0, dyp)
    ax_m.wait_recv()
    axf_m = pass_on(xp * 4 + y, a1, dxm)
    by_m.wait_recv()
    byf_m = pass_on(x * 4 + yp, b1, dym)
    ay[3] = (pass_on(xm * 4 + y, a, dyp), pass_on(xm * 4 + y, a, dym))
    bx[3] = (pass_on(x * 4 + ym, b, dxp), pass_on(x * 4 + ym, b, dxm))
    ay[1] = (pass_on(xp * 4 + y, a, dyp), pass_on(xp * 4 + y, a, dym))
    bx[1] = (pass_on(x * 4 + yp, b, dxp), pass_on(x * 4 + yp, b, dxm))
    last = []

    def relay(k):
        p, m = ay[k]
        xs = (x + k) % 4
        p.wait_recv()
        last.append(pass_on(xs * 4 + ym, a0, dyp))
        m.wait_recv()
        last.append(pass_on(xs * 4 + yp, a1, dym))
        p, m = bx[k]
        ys = (y + k) % 4
        p.wait_recv()
        last.append(pass_on(xm * 4 + ys, b0, dxp))
        m.wait_recv()
        last.append(pass_on(xp * 4 + ys, b1, dxm))

    relay(0)
    axf_p.wait_recv()
    axf_m.wait_recv()
    byf_p.wait_recv()
    byf_m.wait_recv()
    ay[2] = (pass_on(x2 * 4 + y, a, dyp), pass_on(x2 * 4 + y, a, dym))
    bx[2] = (pass_on(x * 4 + y2, b, dxp), pass_on(x * 4 + y2, b, dxm))
    relay(3)
    relay(1)
    relay(2)
    for copy in last:
        copy.wait_recv()
    swap.wait_recv()
    send.finish()
    send2.finish()
    local.wait()


def combine(o4, st, w):
    return pl.pallas_call(
        combine_kernel,
        name="combine",
        out_shape=(
            jax.ShapeDtypeStruct((16, TOK, HEADS * HD), jnp.bfloat16),
            jax.ShapeDtypeStruct(w.shape, jnp.bfloat16),
        ),
        in_specs=[pl.BlockSpec(memory_space=pltpu.VMEM)] * 3,
        out_specs=[pl.BlockSpec(memory_space=pltpu.VMEM)] * 2,
        scratch_shapes=[
            pltpu.VMEM((3, TOK, HEADS * HD), jnp.bfloat16),
            pltpu.VMEM((3, HEADS, TOK), jnp.float32),
            pltpu.VMEM((2, TOK // 2, HEADS * HD), jnp.bfloat16),
            pltpu.VMEM((TOK, HEADS * HD), jnp.bfloat16),
            pltpu.SemaphoreType.DMA((COMBINE_COPIES,)),
            pltpu.SemaphoreType.DMA((COMBINE_COPIES,)),
            pltpu.SemaphoreType.DMA((PLANE_COPIES + 2,)),
            pltpu.SemaphoreType.DMA((PLANE_COPIES + 2,)),
            pltpu.SemaphoreType.DMA((1,)),
        ],
        compiler_params=pltpu.CompilerParams(
            collective_id=1, has_side_effects=True, vmem_limit_bytes=24 << 20
        ),
    )(o4, st, w)


BLK = 512
COLS = 256


def project_kernel(
    att_ref, w_ref, wz_ref, out_ref, give, keep, got, box, core_s, core_r, z_s, z_r
):
    z, x, y = coords()
    tp = lax.axis_index("tp")
    core = tp % 2
    high = tp // 2
    other = {"tp": tp + 1 - 2 * core}
    pos = 2 * high + z
    column = []
    for d in range(1, 8):
        q = (pos + d) % 8
        column.append({"ctx": ctx_of(q % 2, x, y), "tp": (q // 2) * 2 + core})
    entry_barrier(column + [other])

    def product(block, weights):
        rows = att_ref[pl.ds(4 * block, 4)].reshape(BLK, HEADS * HD)
        return jnp.dot(rows, weights[...], preferred_element_type=jnp.float32)

    copies = []
    for upper in range(2):
        block = 2 * upper + 1 - core
        for far in range(2):
            n = 2 * upper + far
            give[n] = product(block, wz_ref if far else w_ref).astype(jnp.bfloat16)
            copy = pltpu.make_async_remote_copy(
                src_ref=give.at[n],
                dst_ref=got.at[n],
                send_sem=core_s.at[n],
                recv_sem=core_r.at[n],
                device_id=other,
                device_id_type=MESH,
            )
            copy.start()
            copies.append(copy)
    for upper in range(2):
        block = 2 * upper + core
        for far in range(2):
            n = 2 * upper + far
            mine = product(block, wz_ref if far else w_ref)
            copies[n].wait()
            keep[n] = (mine + got[n].astype(jnp.float32)).astype(jnp.bfloat16)
            dest_high = 2 * z + upper
            dest_z = 1 - z if far else z
            dest = {"ctx": ctx_of(dest_z, x, y), "tp": dest_high * 2 + core}
            remote = jnp.logical_or(dest_high != high, dest_z != z)

            @pl.when(remote)
            def _(n=n, dest=dest):
                pltpu.make_async_remote_copy(
                    src_ref=keep.at[n],
                    dst_ref=box.at[high],
                    send_sem=z_s.at[n],
                    recv_sem=z_r.at[high],
                    device_id=dest,
                    device_id_type=MESH,
                ).start()

            @pl.when(jnp.logical_not(remote))
            def _(n=n):
                box[high] = keep[n]

    source_z = high // 2
    for s in range(4):
        arrives = jnp.logical_or(high != s, z != source_z)

        @pl.when(arrives)
        def _(s=s):
            pltpu.make_async_remote_copy(
                src_ref=keep.at[0],
                dst_ref=box.at[s],
                send_sem=z_s.at[0],
                recv_sem=z_r.at[s],
                device_id=other,
                device_id_type=MESH,
            ).wait_recv()

    out = box[0].astype(jnp.float32) + box[1].astype(jnp.float32)
    out += box[2].astype(jnp.float32) + box[3].astype(jnp.float32)
    out_ref[...] = out.astype(jnp.bfloat16)
    for upper in range(2):
        for far in range(2):
            n = 2 * upper + far
            remote = jnp.logical_or(2 * z + upper != high, jnp.bool_(far == 1))

            @pl.when(remote)
            def _(n=n):
                pltpu.make_async_remote_copy(
                    src_ref=keep.at[n],
                    dst_ref=box.at[0],
                    send_sem=z_s.at[n],
                    recv_sem=z_r.at[0],
                    device_id=other,
                    device_id_type=MESH,
                ).wait_send()


def project(att, w, wz):
    return pl.pallas_call(
        project_kernel,
        name="project",
        out_shape=jax.ShapeDtypeStruct((BLK, COLS), jnp.bfloat16),
        in_specs=[pl.BlockSpec(memory_space=pltpu.VMEM)] * 3,
        out_specs=pl.BlockSpec(memory_space=pltpu.VMEM),
        scratch_shapes=[
            pltpu.VMEM((4, BLK, COLS), jnp.bfloat16),
            pltpu.VMEM((4, BLK, COLS), jnp.bfloat16),
            pltpu.VMEM((4, BLK, COLS), jnp.bfloat16),
            pltpu.VMEM((4, BLK, COLS), jnp.bfloat16),
            pltpu.SemaphoreType.DMA((4,)),
            pltpu.SemaphoreType.DMA((4,)),
            pltpu.SemaphoreType.DMA((4,)),
            pltpu.SemaphoreType.DMA((4,)),
        ],
        compiler_params=pltpu.CompilerParams(
            collective_id=2, has_side_effects=True, vmem_limit_bytes=24 << 20
        ),
    )(att, w, wz)


def body(queries, span_kv, cache_kv, out_weight, offset, lengths):
    first_token = lax.axis_index("ctx") * TOK
    positions = offset[0] + first_token + jnp.arange(TOK, dtype=jnp.int32)
    rotated = rotate(queries.reshape(TOK, HEADS, HD).astype(jnp.float32), positions)
    rotated = rotated.astype(jnp.bfloat16).reshape(TOK, HEADS * HD)
    keys = rotate(span_kv[:, :, 0, :].astype(jnp.float32), positions).astype(jnp.bfloat16)
    span = jnp.concatenate([keys[:, 0, :], span_kv[:, 0, 1, :]], axis=1)
    kv = jnp.concatenate([cache_kv.reshape(CACHE_ROWS, 2 * HD), span], axis=0)
    q4, kvg = gather(rotated, kv)
    o4, st = attention(lengths, q4, kvg)
    att, wz = combine(o4, st, out_weight)
    return project(att, out_weight, wz)


def solution(mesh):
    return jax.shard_map(
        body,
        mesh=mesh,
        in_specs=(
            P("ctx", "tp"),
            P("ctx", "tp", None, None),
            P("ctx", "tp", None, None),
            P("tp", "ctx"),
            P(),
            P(),
        ),
        out_specs=P("tp", "ctx"),
        check_vma=False,
    )
```

time: 691 us -> 145 us (0.21)
  the two profiles are of different devices: /device:TPU:1 before, /device:TPU:96 now
where the time goes in v1:
time: 145 us
  Pallas kernels  134 us (92%)
  local copies, waits for them, and re-layouts  7.33 us (5%)
  other arithmetic  2.15 us (1%)
    pallas_call x1, Pallas kernels, combine(): pl.pallas_call(combine_kernel, name='combine', out_shape=(jax.ShapeDtypeS...  43.2 us
    pallas_call x1, Pallas kernels, project(): pl.pallas_call(project_kernel, name='project', out_shape=jax.ShapeDtypeSt...  39.4 us
    pallas_call x1, Pallas kernels, attention(): pl.pallas_call(attention_kernel, name='attention', out_shape=(jax.ShapeDt...  26 us
    pallas_call x1, Pallas kernels, gather(): pl.pallas_call(gather_kernel, name='gather_qkv', out_shape=(jax.ShapeDtyp...  25.8 us
    unnamed x15, local copies, waits for them, and re-layouts  6.3 us

profile of v1, /device:TPU:96, one launch (start us, length us, event | category | flops | bytes accessed | tf_op | source)
XLA Modules:
  0.0 144.7 jit_solution(14921602011339673858)
XLA Ops:
  0.7 0.3 multiply_cosine_fusion.1
  1.0 1.0 fusion.11
  2.0 0.3 fusion.10
  2.4 1.0 copy.20
  3.4 0.1 maximum_maximum_fusion.kv_ref
  3.5 1.0 convert_bitcast_fusion
  4.5 0.0 copy-start.1
  4.5 0.1 copy.11
  4.6 0.3 subtract_convert_fusion
  4.9 0.1 pad_maximum_fusion
  5.1 25.8 %gather_qkv.1 = (bf16[4,128,1024]{2,1,0:T(8,128)(2,1)S(1)}, bf16[8,640,256]{2,1,0:T(8,128)(2,1)S(1)}) custom-call(bf16[128,1024]{1,0:T(8,128)(2,1)S(1)} %bitcast.26, bf16[640,256]{1,0:T(8,128)(2,1)S(1)} %maximum_maximum_fusion.kv_ref), custom_call_target="tpu_custom_call" | custom-call | tf_op jit(solution)/shard_map/gather_qkv/pallas_call | solution.py:167
  30.9 0.0 copy-start
  30.9 1.5 %copy-done = bf16[8,640,256]{2,1,0:T(8,128)(2,1)} copy-done((bf16[8,640,256]{2,1,0:T(8,128)(2,1)}, bf16[8,640,256]{2,1,0:T(8,128)(2,1)S(1)}, u32[]{:S(2)}) %copy-start) | copy-done | bytes 2621464
  32.4 0.0 copy-start.3
  32.4 1.0 copy-done.3
  33.4 26.0 %attention.1 = (bf16[4,128,1024]{2,1,0:T(8,128)(2,1)}, f32[4,8,128]{2,1,0:T(8,128)}) custom-call(s32[64]{0:T(128)} %lens_ref.1, bf16[4,128,1024]{2,1,0:T(8,128)(2,1)} %copy-done.3, bf16[8,640,256]{2,1,0:T(8,128)(2,1)} %copy-done), custom_call_target="tpu_custom_call" | custom-call | tf_op jit(solution)/shard_map/attention/pallas_call | solution.py:313
  59.4 0.0 copy-done.1
  59.4 0.0 copy-start.2
  59.4 1.2 copy-done.2
  60.6 0.0 copy-start.4
  60.6 0.7 copy-done.4
  61.3 43.2 %combine.1 = (bf16[16,128,1024]{2,1,0:T(8,128)(2,1)S(1)}, bf16[1024,256]{1,0:T(8,128)(2,1)S(1)}) custom-call(bf16[4,128,1024]{2,1,0:T(8,128)(2,1)S(1)} %copy-done.2, f32[4,8,128]{2,1,0:T(8,128)S(1)} %copy-done.4, bf16[1024,256]{1,0:T(8,128)(2,1)S(1)} %copy-done.1), custom_call_target="tpu_custom_call" | custom-call | tf_op jit(solution)/shard_map/combine/pallas_call | solution.py:472
  104.5 39.4 %project.1 = bf16[512,256]{1,0:T(8,128)(2,1)S(1)} custom-call(bf16[16,128,1024]{2,1,0:T(8,128)(2,1)S(1)} %get-tuple-element.15.att_ref, bf16[1024,256]{1,0:T(8,128)(2,1)S(1)} %copy-done.1, bf16[1024,256]{1,0:T(8,128)(2,1)S(1)} %get-tuple-element.16.wz_ref), custom_call_target="tpu_custom_call" | custom-call | tf_op jit(solution)/shard_map/project/pallas_call | solution.py:600
  144.0 0.7 copy.25
  (5 shorter events, 0.1 us)
Async XLA Ops:
  4.5 54.9 %copy-start.1 = (bf16[1024,256]{1,0:T(8,128)(2,1)S(1)}, bf16[1024,256]{1,0:T(8,128)(2,1)}, u32[]{:S(2)}) copy-start(bf16[1024,256]{1,0:T(8,128)(2,1)} %w_ref.3) | copy-start | bytes 1572868
  30.9 1.5 %copy-start = (bf16[8,640,256]{2,1,0:T(8,128)(2,1)}, bf16[8,640,256]{2,1,0:T(8,128)(2,1)S(1)}, u32[]{:S(2)}) copy-start(bf16[8,640,256]{2,1,0:T(8,128)(2,1)S(1)} %get-tuple-element.12.kvg_ref) | copy-start | bytes 7864324
  32.4 1.0 copy-start.3
  59.4 1.2 copy-start.2
  60.6 0.7 copy-start.4

commit v2 on v1

--- a/solution.py
+++ b/solution.py
@@ -339,17 +339,49 @@
     )(lengths, q4, kvg)
 
 
-COMBINE_COPIES = 8
+COMBINE_COPIES = 9
 PLANE_COPIES = 40
-
-
-def combine_kernel(
-    o4_ref, st_ref, w_ref, att_ref, wz_ref, part, stat, fwd, mine, ssem, rsem, ssem2, rsem2, lsem
+BLK = 512
+COLS = 256
+
+
+def combine_project_kernel(
+    o4_ref,
+    st_ref,
+    w_ref,
+    wz_ref,
+    out_ref,
+    att,
+    part,
+    stat,
+    fwd,
+    mine,
+    prod,
+    give,
+    got,
+    keep,
+    box,
+    ssem,
+    rsem,
+    ssem2,
+    rsem2,
+    core_s,
+    core_r,
+    z_s,
+    z_r,
 ):
     z, x, y = coords()
+    tp = lax.axis_index("tp")
+    core = tp % 2
+    high = tp // 2
+    other = {"tp": tp + 1 - 2 * core}
+    pos = 2 * high + z
+    column = []
+    for d in range(1, 8):
+        q = (pos + d) % 8
+        column.append({"ctx": ctx_of(q % 2, x, y), "tp": (q // 2) * 2 + core})
     xp, xm, x2 = (x + 1) % 4, (x + 3) % 4, (x + 2) % 4
     yp, ym, y2 = (y + 1) % 4, (y + 3) % 4, (y + 2) % 4
-    dz = {"ctx": ctx_of(1 - z, x, y)}
     dxp = {"ctx": ctx_of(z, xp, y)}
     dxm = {"ctx": ctx_of(z, xm, y)}
     dyp = {"ctx": ctx_of(z, x, yp)}
@@ -358,21 +390,19 @@
     half = TOK // 2
     t0 = pl.ds(0, half)
     t1 = pl.ds(half, half)
-    entry_barrier([dz, dxp, dxm, dyp, dym, dy2])
+    entry_barrier([dxp, dxm, dyp, dym, dy2, other] + column)
     send = Sender(ssem, rsem)
     far_p = send(o4_ref.at[y2, t0], fwd.at[0], dyp)
     far_m = send(o4_ref.at[y2, t1], fwd.at[1], dym)
-    to_p = send(o4_ref.at[yp], part.at[2], dyp)
-    to_m = send(o4_ref.at[ym], part.at[0], dym)
     st_p = send(st_ref.at[yp], stat.at[2], dyp)
     st_m = send(st_ref.at[ym], stat.at[0], dym)
     st_2 = send(st_ref.at[y2], stat.at[1], dy2)
-    swap = send(w_ref, wz_ref, dz)
-    send2 = Sender(ssem2, rsem2)
+    to_p = send(o4_ref.at[yp], part.at[2], dyp)
+    to_m = send(o4_ref.at[ym], part.at[0], dym)
     far_p.wait_recv()
-    fw_p = send2(fwd.at[0], part.at[1, t0], dyp)
+    fw_p = send(fwd.at[0], part.at[1, t0], dyp)
     far_m.wait_recv()
-    fw_m = send2(fwd.at[1], part.at[1, t1], dym)
+    fw_m = send(fwd.at[1], part.at[1, t1], dym)
     for copy in (st_p, st_m, st_2):
         copy.wait_recv()
     s_own = st_ref[y]
@@ -389,6 +419,7 @@
     ).T
     for copy in (to_p, to_m, fw_p, fw_m):
         copy.wait_recv()
+    own = x * 4 + y
     for h in range(HEADS):
         lanes = slice(h * HD, (h + 1) * HD)
         out = o4_ref[y, :, lanes].astype(jnp.float32) * table[:, h : h + 1]
@@ -397,31 +428,21 @@
         out += part[1, :, lanes].astype(jnp.float32) * table[:, 24 + h : 25 + h]
         mine[:, lanes] = out.astype(jnp.bfloat16)
 
-    own = x * 4 + y
-    local = pltpu.make_async_copy(mine, att_ref.at[own], lsem.at[0])
-    local.start()
-
+    send2 = Sender(ssem2, rsem2)
     quarter = half // 2
     a, a0, a1 = t0, pl.ds(0, quarter), pl.ds(quarter, quarter)
     b, b0, b1 = t1, pl.ds(half, quarter), pl.ds(half + quarter, quarter)
 
     def pass_on(slot, rows, device):
-        return send2(att_ref.at[slot, rows], att_ref.at[slot, rows], device)
-
-    ax_p = send2(mine.at[a], att_ref.at[own, a], dxp)
-    ax_m = send2(mine.at[a], att_ref.at[own, a], dxm)
-    by_p = send2(mine.at[b], att_ref.at[own, b], dyp)
-    by_m = send2(mine.at[b], att_ref.at[own, b], dym)
-    ay = {}
-    bx = {}
-    ay[0] = (
-        send2(mine.at[a], att_ref.at[own, a], dyp),
-        send2(mine.at[a], att_ref.at[own, a], dym),
-    )
-    bx[0] = (
-        send2(mine.at[b], att_ref.at[own, b], dxp),
-        send2(mine.at[b], att_ref.at[own, b], dxm),
-    )
+        return send2(att.at[slot, rows], att.at[slot, rows], device)
+
+    ax_p = send2(mine.at[a], att.at[own, a], dxp)
+    ax_m = send2(mine.at[a], att.at[own, a], dxm)
+    by_p = send2(mine.at[b], att.at[own, b], dyp)
+    by_m = send2(mine.at[b], att.at[own, b], dym)
+    ay = {0: (send2(mine.at[a], att.at[own, a], dyp), send2(mine.at[a], att.at[own, a], dym))}
+    bx = {0: (send2(mine.at[b], att.at[own, b], dxp), send2(mine.at[b], att.at[own, b], dxm))}
+    att[own] = mine[...]
     ax_p.wait_recv()
     axf_p = pass_on(xm * 4 + y, a0, dxp)
     by_p.wait_recv()
@@ -434,132 +455,103 @@
     bx[3] = (pass_on(x * 4 + ym, b, dxp), pass_on(x * 4 + ym, b, dxm))
     ay[1] = (pass_on(xp * 4 + y, a, dyp), pass_on(xp * 4 + y, a, dym))
     bx[1] = (pass_on(x * 4 + yp, b, dxp), pass_on(x * 4 + yp, b, dxm))
-    last = []
+    last = {}
 
     def relay(k):
         p, m = ay[k]
         xs = (x + k) % 4
         p.wait_recv()
-        last.append(pass_on(xs * 4 + ym, a0, dyp))
+        first = pass_on(xs * 4 + ym, a0, dyp)
         m.wait_recv()
-        last.append(pass_on(xs * 4 + yp, a1, dym))
+        second = pass_on(xs * 4 + yp, a1, dym)
         p, m = bx[k]
         ys = (y + k) % 4
         p.wait_recv()
-        last.append(pass_on(xm * 4 + ys, b0, dxp))
+        third = pass_on(xm * 4 + ys, b0, dxp)
         m.wait_recv()
-        last.append(pass_on(xp * 4 + ys, b1, dxm))
+        fourth = pass_on(xp * 4 + ys, b1, dxm)
+        last[k] = (first, second, third, fourth)
+
+    def wait_all(copies):
+        for copy in copies:
+            copy.wait_recv()
+
+    def row_copies(row, n):
+        core_copy = pltpu.make_async_remote_copy(
+            src_ref=give.at[n],
+            dst_ref=got.at[n],
+            send_sem=core_s.at[n],
+            recv_sem=core_r.at[n],
+            device_id=other,
+            device_id_type=MESH,
+        )
+        out = []
+        for far in range(2):
+            dest_high = 2 * z + row // 2
+            dest_z = 1 - z if far else z
+            copy = pltpu.make_async_remote_copy(
+                src_ref=keep.at[n, far],
+                dst_ref=box.at[high],
+                send_sem=z_s.at[2 * n + far],
+                recv_sem=z_r.at[high],
+                device_id={"ctx": ctx_of(dest_z, x, y), "tp": dest_high * 2 + core},
+                device_id_type=MESH,
+            )
+            remote = (dest_high != high) if far == 0 else None
+            out.append((copy, remote))
+        return core_copy, out
+
+    def product(row, n):
+        keeps = row % 2 == core
+        core_copy, _ = row_copies(row, n)
+        rows = att[pl.ds(4 * row, 4)].reshape(BLK, HEADS * HD)
+        for far, weights in enumerate((w_ref, wz_ref)):
+            prod[n % 2, far] = jnp.dot(rows, weights[...], preferred_element_type=jnp.float32)
+
+        @pl.when(jnp.logical_not(keeps))
+        def _():
+            give[n] = prod[n % 2].astype(jnp.bfloat16)
+            core_copy.start()
+
+    def settle(row, n):
+        keeps = row % 2 == core
+        core_copy, copies = row_copies(row, n)
+
+        @pl.when(keeps)
+        def _():
+            core_copy.wait_recv()
+            keep[n] = (prod[n % 2] + got[n].astype(jnp.float32)).astype(jnp.bfloat16)
+            for far, (copy, remote) in enumerate(copies):
+                if remote is None:
+                    copy.start()
+                else:
+                    pl.when(remote)(copy.start)
+
+                    @pl.when(jnp.logical_not(remote))
+                    def _():
+                        box[high] = keep[n, far]
 
     relay(0)
-    axf_p.wait_recv()
-    axf_m.wait_recv()
-    byf_p.wait_recv()
-    byf_m.wait_recv()
+    wait_all((axf_p, axf_m, byf_p, byf_m))
     ay[2] = (pass_on(x2 * 4 + y, a, dyp), pass_on(x2 * 4 + y, a, dym))
     bx[2] = (pass_on(x * 4 + y2, b, dxp), pass_on(x * 4 + y2, b, dxm))
+    wait_all(last[0][:2])
+    product(x, 0)
     relay(3)
+    settle(x, 0)
     relay(1)
     relay(2)
-    for copy in last:
-        copy.wait_recv()
-    swap.wait_recv()
-    send.finish()
-    send2.finish()
-    local.wait()
-
-
-def combine(o4, st, w):
-    return pl.pallas_call(
-        combine_kernel,
-        name="combine",
-        out_shape=(
-            jax.ShapeDtypeStruct((16, TOK, HEADS * HD), jnp.bfloat16),
-            jax.ShapeDtypeStruct(w.shape, jnp.bfloat16),
-        ),
-        in_specs=[pl.BlockSpec(memory_space=pltpu.VMEM)] * 3,
-        out_specs=[pl.BlockSpec(memory_space=pltpu.VMEM)] * 2,
-        scratch_shapes=[
-            pltpu.VMEM((3, TOK, HEADS * HD), jnp.bfloat16),
-            pltpu.VMEM((3, HEADS, TOK), jnp.float32),
-            pltpu.VMEM((2, TOK // 2, HEADS * HD), jnp.bfloat16),
-            pltpu.VMEM((TOK, HEADS * HD), jnp.bfloat16),
-            pltpu.SemaphoreType.DMA((COMBINE_COPIES,)),
-            pltpu.SemaphoreType.DMA((COMBINE_COPIES,)),
-            pltpu.SemaphoreType.DMA((PLANE_COPIES + 2,)),
-            pltpu.SemaphoreType.DMA((PLANE_COPIES + 2,)),
-            pltpu.SemaphoreType.DMA((1,)),
-        ],
-        compiler_params=pltpu.CompilerParams(
-            collective_id=1, has_side_effects=True, vmem_limit_bytes=24 << 20
-        ),
-    )(o4, st, w)
-
-
-BLK = 512
-COLS = 256
-
-
-def project_kernel(
-    att_ref, w_ref, wz_ref, out_ref, give, keep, got, box, core_s, core_r, z_s, z_r
-):
-    z, x, y = coords()
-    tp = lax.axis_index("tp")
-    core = tp % 2
-    high = tp // 2
-    other = {"tp": tp + 1 - 2 * core}
-    pos = 2 * high + z
-    column = []
-    for d in range(1, 8):
-        q = (pos + d) % 8
-        column.append({"ctx": ctx_of(q % 2, x, y), "tp": (q // 2) * 2 + core})
-    entry_barrier(column + [other])
-
-    def product(block, weights):
-        rows = att_ref[pl.ds(4 * block, 4)].reshape(BLK, HEADS * HD)
-        return jnp.dot(rows, weights[...], preferred_element_type=jnp.float32)
-
-    copies = []
-    for upper in range(2):
-        block = 2 * upper + 1 - core
-        for far in range(2):
-            n = 2 * upper + far
-            give[n] = product(block, wz_ref if far else w_ref).astype(jnp.bfloat16)
-            copy = pltpu.make_async_remote_copy(
-                src_ref=give.at[n],
-                dst_ref=got.at[n],
-                send_sem=core_s.at[n],
-                recv_sem=core_r.at[n],
-                device_id=other,
-                device_id_type=MESH,
-            )
-            copy.start()
-            copies.append(copy)
-    for upper in range(2):
-        block = 2 * upper + core
-        for far in range(2):
-            n = 2 * upper + far
-            mine = product(block, wz_ref if far else w_ref)
-            copies[n].wait()
-            keep[n] = (mine + got[n].astype(jnp.float32)).astype(jnp.bfloat16)
-            dest_high = 2 * z + upper
-            dest_z = 1 - z if far else z
-            dest = {"ctx": ctx_of(dest_z, x, y), "tp": dest_high * 2 + core}
-            remote = jnp.logical_or(dest_high != high, dest_z != z)
-
-            @pl.when(remote)
-            def _(n=n, dest=dest):
-                pltpu.make_async_remote_copy(
-                    src_ref=keep.at[n],
-                    dst_ref=box.at[high],
-                    send_sem=z_s.at[n],
-                    recv_sem=z_r.at[high],
-                    device_id=dest,
-                    device_id_type=MESH,
-                ).start()
-
-            @pl.when(jnp.logical_not(remote))
-            def _(n=n):
-                box[high] = keep[n]
+    wait_all(last[3][:2])
+    product(xm, 1)
+    settle(xm, 1)
+    wait_all(last[1][:2])
+    product(xp, 2)
+    settle(xp, 2)
+    wait_all(last[2][:2])
+    for k in range(4):
+        wait_all(last[k][2:])
+    product(x2, 3)
+    settle(x2, 3)
 
     source_z = high // 2
     for s in range(4):
@@ -568,7 +560,7 @@
         @pl.when(arrives)
         def _(s=s):
             pltpu.make_async_remote_copy(
-                src_ref=keep.at[0],
+                src_ref=keep.at[0, 0],
                 dst_ref=box.at[s],
                 send_sem=z_s.at[0],
                 recv_sem=z_r.at[s],
@@ -576,47 +568,57 @@
                 device_id_type=MESH,
             ).wait_recv()
 
-    out = box[0].astype(jnp.float32) + box[1].astype(jnp.float32)
-    out += box[2].astype(jnp.float32) + box[3].astype(jnp.float32)
-    out_ref[...] = out.astype(jnp.bfloat16)
-    for upper in range(2):
-        for far in range(2):
-            n = 2 * upper + far
-            remote = jnp.logical_or(2 * z + upper != high, jnp.bool_(far == 1))
-
-            @pl.when(remote)
-            def _(n=n):
-                pltpu.make_async_remote_copy(
-                    src_ref=keep.at[n],
-                    dst_ref=box.at[0],
-                    send_sem=z_s.at[n],
-                    recv_sem=z_r.at[0],
-                    device_id=other,
-                    device_id_type=MESH,
-                ).wait_send()
-
-
-def project(att, w, wz):
+    total = box[0].astype(jnp.float32) + box[1].astype(jnp.float32)
+    total += box[2].astype(jnp.float32) + box[3].astype(jnp.float32)
+    out_ref[...] = total.astype(jnp.bfloat16)
+    for n, row in enumerate((x, xm, xp, x2)):
+        keeps = row % 2 == core
+        core_copy, copies = row_copies(row, n)
+
+        @pl.when(keeps)
+        def _(copies=copies):
+            for copy, remote in copies:
+                if remote is None:
+                    copy.wait_send()
+                else:
+                    pl.when(remote)(copy.wait_send)
+
+        pl.when(jnp.logical_not(keeps))(core_copy.wait_send)
+    send.finish()
+    send2.finish()
+
+
+def combine_project(o4, st, w, wz):
     return pl.pallas_call(
-        project_kernel,
-        name="project",
+        combine_project_kernel,
+        name="combine_project",
         out_shape=jax.ShapeDtypeStruct((BLK, COLS), jnp.bfloat16),
-        in_specs=[pl.BlockSpec(memory_space=pltpu.VMEM)] * 3,
+        in_specs=[pl.BlockSpec(memory_space=pltpu.VMEM)] * 4,
         out_specs=pl.BlockSpec(memory_space=pltpu.VMEM),
         scratch_shapes=[
+            pltpu.VMEM((16, TOK, HEADS * HD), jnp.bfloat16),
+            pltpu.VMEM((3, TOK, HEADS * HD), jnp.bfloat16),
+            pltpu.VMEM((3, HEADS, TOK), jnp.float32),
+            pltpu.VMEM((2, TOK // 2, HEADS * HD), jnp.bfloat16),
+            pltpu.VMEM((TOK, HEADS * HD), jnp.bfloat16),
+            pltpu.VMEM((2, 2, BLK, COLS), jnp.float32),
+            pltpu.VMEM((4, 2, BLK, COLS), jnp.bfloat16),
+            pltpu.VMEM((4, 2, BLK, COLS), jnp.bfloat16),
+            pltpu.VMEM((4, 2, BLK, COLS), jnp.bfloat16),
             pltpu.VMEM((4, BLK, COLS), jnp.bfloat16),
-            pltpu.VMEM((4, BLK, COLS), jnp.bfloat16),
-            pltpu.VMEM((4, BLK, COLS), jnp.bfloat16),
-            pltpu.VMEM((4, BLK, COLS), jnp.bfloat16),
+            pltpu.SemaphoreType.DMA((COMBINE_COPIES,)),
+            pltpu.SemaphoreType.DMA((COMBINE_COPIES,)),
+            pltpu.SemaphoreType.DMA((PLANE_COPIES,)),
+            pltpu.SemaphoreType.DMA((PLANE_COPIES,)),
             pltpu.SemaphoreType.DMA((4,)),
             pltpu.SemaphoreType.DMA((4,)),
-            pltpu.SemaphoreType.DMA((4,)),
+            pltpu.SemaphoreType.DMA((8,)),
             pltpu.SemaphoreType.DMA((4,)),
         ],
         compiler_params=pltpu.CompilerParams(
-            collective_id=2, has_side_effects=True, vmem_limit_bytes=24 << 20
+            collective_id=1, has_side_effects=True, vmem_limit_bytes=32 << 20
         ),
-    )(att, w, wz)
+    )(o4, st, w, wz)
 
 
 def body(queries, span_kv, cache_kv, out_weight, offset, lengths):
@@ -627,10 +629,10 @@
     keys = rotate(span_kv[:, :, 0, :].astype(jnp.float32), positions).astype(jnp.bfloat16)
     span = jnp.concatenate([keys[:, 0, :], span_kv[:, 0, 1, :]], axis=1)
     kv = jnp.concatenate([cache_kv.reshape(CACHE_ROWS, 2 * HD), span], axis=0)
+    wz = lax.ppermute(out_weight, "ctx", [(c, (c + 16) % 32) for c in range(32)])
     q4, kvg = gather(rotated, kv)
     o4, st = attention(lengths, q4, kvg)
-    att, wz = combine(o4, st, out_weight)
-    return project(att, out_weight, wz)
+    return combine_project(o4, st, out_weight, wz)
 
 
 def solution(mesh):

time: 145 us -> 142 us (0.979)
  the two profiles are of different devices: /device:TPU:96 before, /device:TPU:1 now
where the time goes in v2:
time: 142 us
  Pallas kernels  131 us (92%)
  local copies, waits for them, and re-layouts  5.42 us (4%)
  starting transfers between devices  2.47 us (2%)
  other arithmetic  2.19 us (2%)
    pallas_call x1, Pallas kernels, combine_project(): pl.pallas_call(combine_project_kernel, name='combine_project', out_shape=...  79.7 us
    pallas_call x1, Pallas kernels, attention(): pl.pallas_call(attention_kernel, name='attention', out_shape=(jax.ShapeDt...  25.9 us
    pallas_call x1, Pallas kernels, gather(): pl.pallas_call(gather_kernel, name='gather_qkv', out_shape=(jax.ShapeDtyp...  25.5 us
    unnamed x19, local copies, waits for them, and re-layouts  5.33 us
  transfers between devices with their start and end apart: 1, of which 0 were waited for; matrix products, arithmetic and copies ran while one was open for 2% of the time, Pallas kernels for 36%

profile of v2, /device:TPU:1, one launch (start us, length us, event | category | flops | bytes accessed | tf_op | source)
XLA Modules:
  0.0 142.1 jit_solution(906813392588204182)
XLA Ops:
  0.0 0.0 copy-start.6
  0.0 2.5 %collective-permute-start = (bf16[1024,256]{1,0:T(8,128)(2,1)}, bf16[1024,256]{1,0:T(8,128)(2,1)S(1)}, u32[]{:S(2)}, u32[]{:S(2)}) collective-permute-start(bf16[1024,256]{1,0:T(8,128)(2,1)} %w_ref.1), channel_id=1, source_target_pairs={{0,128},{8,136},{16,144},{24,152},{32,160},{40,168},{48,176},{56,1... | collective-permute-start | bytes 1572872 | tf_op jit(solution)/shard_map/ppermute | solution.py:632
  3.1 0.0 copy-start.5
  3.2 1.0 convert_bitcast_fusion
  4.2 0.1 copy.11
  4.3 0.3 multiply_cosine_fusion.1
  4.6 0.3 subtract_convert_fusion
  4.9 0.1 pad_maximum_fusion
  5.1 0.0 copy-done.6
  5.1 0.1 fusion.11
  5.2 0.0 copy-done.5
  5.3 0.0 copy-start.3
  5.3 0.3 fusion.10
  5.6 0.1 maximum_maximum_fusion.kv_ref
  5.7 25.5 %gather_qkv.1 = (bf16[4,128,1024]{2,1,0:T(8,128)(2,1)S(1)}, bf16[8,640,256]{2,1,0:T(8,128)(2,1)S(1)}) custom-call(bf16[128,1024]{1,0:T(8,128)(2,1)S(1)} %bitcast.26, bf16[640,256]{1,0:T(8,128)(2,1)S(1)} %maximum_maximum_fusion.kv_ref), custom_call_target="tpu_custom_call" | custom-call | tf_op jit(solution)/shard_map/gather_qkv/pallas_call | solution.py:167
  31.3 0.0 copy-start
  31.3 1.5 %copy-done = bf16[8,640,256]{2,1,0:T(8,128)(2,1)} copy-done((bf16[8,640,256]{2,1,0:T(8,128)(2,1)}, bf16[8,640,256]{2,1,0:T(8,128)(2,1)S(1)}, u32[]{:S(2)}) %copy-start) | copy-done | bytes 2621464
  32.8 0.0 copy-start.2
  32.8 1.0 copy-done.2
  33.8 25.9 %attention.1 = (bf16[4,128,1024]{2,1,0:T(8,128)(2,1)}, f32[4,8,128]{2,1,0:T(8,128)}) custom-call(s32[64]{0:T(128)} %lens_ref.1, bf16[4,128,1024]{2,1,0:T(8,128)(2,1)} %copy-done.2, bf16[8,640,256]{2,1,0:T(8,128)(2,1)} %copy-done), custom_call_target="tpu_custom_call" | custom-call | tf_op jit(solution)/shard_map/attention/pallas_call | solution.py:313
  59.7 0.0 collective-permute-done.wz_ref
  59.7 0.0 copy-done.3
  59.7 0.0 copy-start.1
  59.8 1.2 copy-done.1
  61.0 0.0 copy-start.4
  61.0 0.7 copy-done.4
  61.7 79.7 %combine_project.1 = bf16[512,256]{1,0:T(8,128)(2,1)S(1)} custom-call(bf16[4,128,1024]{2,1,0:T(8,128)(2,1)S(1)} %copy-done.1, f32[4,8,128]{2,1,0:T(8,128)S(1)} %copy-done.4, bf16[1024,256]{1,0:T(8,128)(2,1)S(1)} %copy-done.3, bf16[1024,256]{1,0:T(8,128)(2,1)S(1)} %collective-permute-done.wz_ref), custom_call_target="tpu_custom_call" | custom-call | tf_op jit(solution)/shard_map/combine_project/pallas_call | solution.py:592
  141.4 0.7 copy.25
  (6 shorter events, 0.1 us)
Async XLA Ops:
  0.0 5.1 %copy-start.6 = (bf16[128,1,2,128]{3,2,1,0:T(2,128)(2,1)S(1)}, bf16[128,1,2,128]{3,2,1,0:T(2,128)(2,1)}, u32[]{:S(2)}) copy-start(bf16[128,1,2,128]{3,2,1,0:T(2,128)(2,1)} %param.7) | copy-start | bytes 196612
  0.0 59.7 %collective-permute-start = (bf16[1024,256]{1,0:T(8,128)(2,1)}, bf16[1024,256]{1,0:T(8,128)(2,1)S(1)}, u32[]{:S(2)}, u32[]{:S(2)}) collective-permute-start(bf16[1024,256]{1,0:T(8,128)(2,1)} %w_ref.1), channel_id=1, source_target_pairs={{0,128},{8,136},{16,144},{24,152},{32,160},{40,168},{48,176},{56,1... | collective-permute-start | bytes 1572872 | tf_op jit(solution)/shard_map/ppermute | solution.py:632
  3.1 2.1 %copy-start.5 = (bf16[512,1,2,128]{3,2,1,0:T(2,128)(2,1)S(1)}, bf16[512,1,2,128]{3,2,1,0:T(2,128)(2,1)}, u32[]{:S(2)}) copy-start(bf16[512,1,2,128]{3,2,1,0:T(2,128)(2,1)} %param.8) | copy-start | bytes 786436
  5.3 54.5 %copy-start.3 = (bf16[1024,256]{1,0:T(8,128)(2,1)S(1)}, bf16[1024,256]{1,0:T(8,128)(2,1)}, u32[]{:S(2)}) copy-start(bf16[1024,256]{1,0:T(8,128)(2,1)} %w_ref.1) | copy-start | bytes 1572868
  31.3 1.5 %copy-start = (bf16[8,640,256]{2,1,0:T(8,128)(2,1)}, bf16[8,640,256]{2,1,0:T(8,128)(2,1)S(1)}, u32[]{:S(2)}) copy-start(bf16[8,640,256]{2,1,0:T(8,128)(2,1)S(1)} %get-tuple-element.10.kvg_ref) | copy-start | bytes 7864324
  32.8 1.0 copy-start.2
  59.7 1.2 copy-start.1
  61.0 0.7 copy-start.4

commit v3 on v2

--- a/solution.py
+++ b/solution.py
@@ -350,12 +350,15 @@
     st_ref,
     w_ref,
     wz_ref,
+    wh_ref,
+    wzh_ref,
     out_ref,
     att,
     part,
     stat,
+    table,
     fwd,
-    mine,
+    away,
     prod,
     give,
     got,
@@ -374,7 +377,9 @@
     tp = lax.axis_index("tp")
     core = tp % 2
     high = tp // 2
+    even = high % 2
     other = {"tp": tp + 1 - 2 * core}
+    pair = {"tp": tp + 2 - 4 * even}
     pos = 2 * high + z
     column = []
     for d in range(1, 8):
@@ -413,71 +418,74 @@
     e_m = jnp.exp2(s_m - top)
     e_2 = jnp.exp2(s_2 - top)
     norm = 1.0 / (e_own + e_p + e_m + e_2)
-    table = jnp.concatenate(
+    table[...] = jnp.concatenate(
         [e_own * norm, e_p * norm, e_m * norm, e_2 * norm, jnp.zeros((96, TOK), jnp.float32)],
         axis=0,
     ).T
     for copy in (to_p, to_m, fw_p, fw_m):
         copy.wait_recv()
     own = x * 4 + y
-    for h in range(HEADS):
-        lanes = slice(h * HD, (h + 1) * HD)
-        out = o4_ref[y, :, lanes].astype(jnp.float32) * table[:, h : h + 1]
-        out += part[0, :, lanes].astype(jnp.float32) * table[:, 8 + h : 9 + h]
-        out += part[2, :, lanes].astype(jnp.float32) * table[:, 16 + h : 17 + h]
-        out += part[1, :, lanes].astype(jnp.float32) * table[:, 24 + h : 25 + h]
-        mine[:, lanes] = out.astype(jnp.bfloat16)
+
+    def combined(first, dest):
+        rows = pl.ds(pl.multiple_of(first, half), half)
+        for h in range(HEADS):
+            lanes = slice(h * HD, (h + 1) * HD)
+            out = o4_ref[y, rows, lanes].astype(jnp.float32) * table[rows, h : h + 1]
+            out += part[0, rows, lanes].astype(jnp.float32) * table[rows, 8 + h : 9 + h]
+            out += part[2, rows, lanes].astype(jnp.float32) * table[rows, 16 + h : 17 + h]
+            out += part[1, rows, lanes].astype(jnp.float32) * table[rows, 24 + h : 25 + h]
+            dest[:, lanes] = out.astype(jnp.bfloat16)
 
     send2 = Sender(ssem2, rsem2)
+    combined((1 - even) * half, away)
+    swap = send2(away, att.at[1, own], pair)
+    combined(even * half, att.at[0, own])
     quarter = half // 2
-    a, a0, a1 = t0, pl.ds(0, quarter), pl.ds(quarter, quarter)
-    b, b0, b1 = t1, pl.ds(half, quarter), pl.ds(half + quarter, quarter)
-
-    def pass_on(slot, rows, device):
-        return send2(att.at[slot, rows], att.at[slot, rows], device)
-
-    ax_p = send2(mine.at[a], att.at[own, a], dxp)
-    ax_m = send2(mine.at[a], att.at[own, a], dxm)
-    by_p = send2(mine.at[b], att.at[own, b], dyp)
-    by_m = send2(mine.at[b], att.at[own, b], dym)
-    ay = {0: (send2(mine.at[a], att.at[own, a], dyp), send2(mine.at[a], att.at[own, a], dym))}
-    bx = {0: (send2(mine.at[b], att.at[own, b], dxp), send2(mine.at[b], att.at[own, b], dxm))}
-    att[own] = mine[...]
+    lo, hi, full = pl.ds(0, quarter), pl.ds(quarter, quarter), pl.ds(0, half)
+
+    def pass_on(k, slot, rows, device):
+        return send2(att.at[k, slot, rows], att.at[k, slot, rows], device)
+
+    ax_p = pass_on(0, own, full, dxp)
+    ax_m = pass_on(0, own, full, dxm)
+    ay = {0: (pass_on(0, own, full, dyp), pass_on(0, own, full, dym))}
+    bx = {}
     ax_p.wait_recv()
-    axf_p = pass_on(xm * 4 + y, a0, dxp)
-    by_p.wait_recv()
-    byf_p = pass_on(x * 4 + ym, b0, dyp)
+    axf_p = pass_on(0, xm * 4 + y, lo, dxp)
+    ay[3] = (pass_on(0, xm * 4 + y, full, dyp), pass_on(0, xm * 4 + y, full, dym))
     ax_m.wait_recv()
-    axf_m = pass_on(xp * 4 + y, a1, dxm)
-    by_m.wait_recv()
-    byf_m = pass_on(x * 4 + yp, b1, dym)
-    ay[3] = (pass_on(xm * 4 + y, a, dyp), pass_on(xm * 4 + y, a, dym))
-    bx[3] = (pass_on(x * 4 + ym, b, dxp), pass_on(x * 4 + ym, b, dxm))
-    ay[1] = (pass_on(xp * 4 + y, a, dyp), pass_on(xp * 4 + y, a, dym))
-    bx[1] = (pass_on(x * 4 + yp, b, dxp), pass_on(x * 4 + yp, b, dxm))
+    axf_m = pass_on(0, xp * 4 + y, hi, dxm)
+    ay[1] = (pass_on(0, xp * 4 + y, full, dyp), pass_on(0, xp * 4 + y, full, dym))
+    swap.wait_recv()
+    by_p = pass_on(1, own, full, dyp)
+    by_m = pass_on(1, own, full, dym)
+    bx[0] = (pass_on(1, own, full, dxp), pass_on(1, own, full, dxm))
     last = {}
 
-    def relay(k):
+    def relay_a(k):
         p, m = ay[k]
         xs = (x + k) % 4
         p.wait_recv()
-        first = pass_on(xs * 4 + ym, a0, dyp)
+        first = pass_on(0, xs * 4 + ym, lo, dyp)
         m.wait_recv()
-        second = pass_on(xs * 4 + yp, a1, dym)
+        second = pass_on(0, xs * 4 + yp, hi, dym)
+        last[0, k] = (first, second)
+
+    def relay_b(k):
         p, m = bx[k]
         ys = (y + k) % 4
         p.wait_recv()
-        third = pass_on(xm * 4 + ys, b0, dxp)
+        third = pass_on(1, xm * 4 + ys, lo, dxp)
         m.wait_recv()
-        fourth = pass_on(xp * 4 + ys, b1, dxm)
-        last[k] = (first, second, third, fourth)
+        fourth = pass_on(1, xp * 4 + ys, hi, dxm)
+        last[1, k] = (third, fourth)
 
     def wait_all(copies):
         for copy in copies:
             copy.wait_recv()
 
-    def row_copies(row, n):
-        core_copy = pltpu.make_async_remote_copy(
+    def core_copy(n):
+        return pltpu.make_async_remote_copy(
             src_ref=give.at[n],
             dst_ref=got.at[n],
             send_sem=core_s.at[n],
@@ -485,71 +493,83 @@
             device_id=other,
             device_id_type=MESH,
         )
-        out = []
-        for far in range(2):
-            dest_high = 2 * z + row // 2
-            dest_z = 1 - z if far else z
-            copy = pltpu.make_async_remote_copy(
-                src_ref=keep.at[n, far],
-                dst_ref=box.at[high],
-                send_sem=z_s.at[2 * n + far],
-                recv_sem=z_r.at[high],
-                device_id={"ctx": ctx_of(dest_z, x, y), "tp": dest_high * 2 + core},
-                device_id_type=MESH,
-            )
-            remote = (dest_high != high) if far == 0 else None
-            out.append((copy, remote))
-        return core_copy, out
+
+    def z_copy(row, n, far):
+        return pltpu.make_async_remote_copy(
+            src_ref=keep.at[n, far],
+            dst_ref=box.at[high],
+            send_sem=z_s.at[2 * n + far],
+            recv_sem=z_r.at[high],
+            device_id={
+                "ctx": ctx_of(1 - z if far else z, x, y),
+                "tp": (2 * z + row // 2) * 2 + core,
+            },
+            device_id_type=MESH,
+        )
 
     def product(row, n):
         keeps = row % 2 == core
-        core_copy, _ = row_copies(row, n)
-        rows = att[pl.ds(4 * row, 4)].reshape(BLK, HEADS * HD)
-        for far, weights in enumerate((w_ref, wz_ref)):
-            prod[n % 2, far] = jnp.dot(rows, weights[...], preferred_element_type=jnp.float32)
+        slots = pl.ds(4 * row, 4)
+        rows_a = att[0, slots].reshape(BLK // 2, HEADS * HD)
+        rows_b = att[1, slots].reshape(BLK // 2, HEADS * HD)
+        for far, (wa, wb) in enumerate(((w_ref, wh_ref), (wz_ref, wzh_ref))):
+            prod[n % 2, far] = jnp.dot(
+                rows_a, wa[...], preferred_element_type=jnp.float32
+            ) + jnp.dot(rows_b, wb[...], preferred_element_type=jnp.float32)
 
         @pl.when(jnp.logical_not(keeps))
         def _():
             give[n] = prod[n % 2].astype(jnp.bfloat16)
-            core_copy.start()
+            core_copy(n).start()
 
     def settle(row, n):
         keeps = row % 2 == core
-        core_copy, copies = row_copies(row, n)
+        remote = 2 * z + row // 2 != high
 
         @pl.when(keeps)
         def _():
-            core_copy.wait_recv()
+            core_copy(n).wait_recv()
             keep[n] = (prod[n % 2] + got[n].astype(jnp.float32)).astype(jnp.bfloat16)
-            for far, (copy, remote) in enumerate(copies):
-                if remote is None:
-                    copy.start()
-                else:
-                    pl.when(remote)(copy.start)
-
-                    @pl.when(jnp.logical_not(remote))
-                    def _():
-                        box[high] = keep[n, far]
-
-    relay(0)
-    wait_all((axf_p, axf_m, byf_p, byf_m))
-    ay[2] = (pass_on(x2 * 4 + y, a, dyp), pass_on(x2 * 4 + y, a, dym))
-    bx[2] = (pass_on(x * 4 + y2, b, dxp), pass_on(x * 4 + y2, b, dxm))
-    wait_all(last[0][:2])
+            z_copy(row, n, 1).start()
+
+            @pl.when(remote)
+            def _():
+                z_copy(row, n, 0).start()
+
+            @pl.when(jnp.logical_not(remote))
+            def _():
+                box[high] = keep[n, 0]
+
+    relay_a(0)
+    by_p.wait_recv()
+    byf_p = pass_on(1, x * 4 + ym, lo, dyp)
+    bx[3] = (pass_on(1, x * 4 + ym, full, dxp), pass_on(1, x * 4 + ym, full, dxm))
+    by_m.wait_recv()
+    byf_m = pass_on(1, x * 4 + yp, hi, dym)
+    bx[1] = (pass_on(1, x * 4 + yp, full, dxp), pass_on(1, x * 4 + yp, full, dxm))
+    wait_all((axf_p, axf_m))
+    ay[2] = (pass_on(0, x2 * 4 + y, full, dyp), pass_on(0, x2 * 4 + y, full, dym))
+    relay_a(3)
+    relay_b(0)
+    wait_all((byf_p, byf_m))
+    bx[2] = (pass_on(1, x * 4 + y2, full, dxp), pass_on(1, x * 4 + y2, full, dxm))
+    wait_all(last[0, 0])
     product(x, 0)
-    relay(3)
+    relay_a(1)
     settle(x, 0)
-    relay(1)
-    relay(2)
-    wait_all(last[3][:2])
+    relay_b(3)
+    relay_b(1)
+    relay_a(2)
+    relay_b(2)
+    wait_all(last[0, 3])
     product(xm, 1)
     settle(xm, 1)
-    wait_all(last[1][:2])
+    wait_all(last[0, 1])
     product(xp, 2)
     settle(xp, 2)
-    wait_all(last[2][:2])
+    wait_all(last[0, 2])
     for k in range(4):
-        wait_all(last[k][2:])
+        wait_all(last[1, k])
     product(x2, 3)
     settle(x2, 3)
 
@@ -568,48 +588,55 @@
                 device_id_type=MESH,
             ).wait_recv()
 
-    total = box[0].astype(jnp.float32) + box[1].astype(jnp.float32)
-    total += box[2].astype(jnp.float32) + box[3].astype(jnp.float32)
-    out_ref[...] = total.astype(jnp.bfloat16)
+    for e in range(2):
+        total = box[e].astype(jnp.float32) + box[2 + e].astype(jnp.float32)
+        total = total.astype(jnp.bfloat16)
+        for g in range(4):
+            first = g * TOK + e * half
+            out_ref[first : first + half] = total[g * half : (g + 1) * half]
     for n, row in enumerate((x, xm, xp, x2)):
         keeps = row % 2 == core
-        core_copy, copies = row_copies(row, n)
+        remote = 2 * z + row // 2 != high
 
         @pl.when(keeps)
-        def _(copies=copies):
-            for copy, remote in copies:
-                if remote is None:
-                    copy.wait_send()
-                else:
-                    pl.when(remote)(copy.wait_send)
-
-        pl.when(jnp.logical_not(keeps))(core_copy.wait_send)
+        def _(n=n, row=row, remote=remote):
+            z_copy(row, n, 1).wait_send()
+
+            @pl.when(remote)
+            def _():
+                z_copy(row, n, 0).wait_send()
+
+        @pl.when(jnp.logical_not(keeps))
+        def _(n=n):
+            core_copy(n).wait_send()
+
     send.finish()
     send2.finish()
 
 
-def combine_project(o4, st, w, wz):
+def combine_project(o4, st, *weights):
     return pl.pallas_call(
         combine_project_kernel,
         name="combine_project",
         out_shape=jax.ShapeDtypeStruct((BLK, COLS), jnp.bfloat16),
-        in_specs=[pl.BlockSpec(memory_space=pltpu.VMEM)] * 4,
+        in_specs=[pl.BlockSpec(memory_space=pltpu.VMEM)] * 6,
         out_specs=pl.BlockSpec(memory_space=pltpu.VMEM),
         scratch_shapes=[
-            pltpu.VMEM((16, TOK, HEADS * HD), jnp.bfloat16),
+            pltpu.VMEM((2, 16, TOK // 2, HEADS * HD), jnp.bfloat16),
             pltpu.VMEM((3, TOK, HEADS * HD), jnp.bfloat16),
             pltpu.VMEM((3, HEADS, TOK), jnp.float32),
+            pltpu.VMEM((TOK, TOK), jnp.float32),
             pltpu.VMEM((2, TOK // 2, HEADS * HD), jnp.bfloat16),
-            pltpu.VMEM((TOK, HEADS * HD), jnp.bfloat16),
-            pltpu.VMEM((2, 2, BLK, COLS), jnp.float32),
-            pltpu.VMEM((4, 2, BLK, COLS), jnp.bfloat16),
-            pltpu.VMEM((4, 2, BLK, COLS), jnp.bfloat16),
-            pltpu.VMEM((4, 2, BLK, COLS), jnp.bfloat16),
-            pltpu.VMEM((4, BLK, COLS), jnp.bfloat16),
+            pltpu.VMEM((TOK // 2, HEADS * HD), jnp.bfloat16),
+            pltpu.VMEM((2, 2, BLK // 2, COLS), jnp.float32),
+            pltpu.VMEM((4, 2, BLK // 2, COLS), jnp.bfloat16),
+            pltpu.VMEM((4, 2, BLK // 2, COLS), jnp.bfloat16),
+            pltpu.VMEM((4, 2, BLK // 2, COLS), jnp.bfloat16),
+            pltpu.VMEM((4, BLK // 2, COLS), jnp.bfloat16),
             pltpu.SemaphoreType.DMA((COMBINE_COPIES,)),
             pltpu.SemaphoreType.DMA((COMBINE_COPIES,)),
-            pltpu.SemaphoreType.DMA((PLANE_COPIES,)),
-            pltpu.SemaphoreType.DMA((PLANE_COPIES,)),
+            pltpu.SemaphoreType.DMA((PLANE_COPIES + 1,)),
+            pltpu.SemaphoreType.DMA((PLANE_COPIES + 1,)),
             pltpu.SemaphoreType.DMA((4,)),
             pltpu.SemaphoreType.DMA((4,)),
             pltpu.SemaphoreType.DMA((8,)),
@@ -618,7 +645,7 @@
         compiler_params=pltpu.CompilerParams(
             collective_id=1, has_side_effects=True, vmem_limit_bytes=32 << 20
         ),
-    )(o4, st, w, wz)
+    )(o4, st, *weights)
 
 
 def body(queries, span_kv, cache_kv, out_weight, offset, lengths):
@@ -629,10 +656,17 @@
     keys = rotate(span_kv[:, :, 0, :].astype(jnp.float32), positions).astype(jnp.bfloat16)
     span = jnp.concatenate([keys[:, 0, :], span_kv[:, 0, 1, :]], axis=1)
     kv = jnp.concatenate([cache_kv.reshape(CACHE_ROWS, 2 * HD), span], axis=0)
-    wz = lax.ppermute(out_weight, "ctx", [(c, (c + 16) % 32) for c in range(32)])
     q4, kvg = gather(rotated, kv)
+    w = lax.optimization_barrier((out_weight, kvg))[0]
+    wz = lax.ppermute(w, "ctx", [(c, (c + 16) % 32) for c in range(32)])
+    swap_pair = [(t, t + 2 - 4 * (t // 2 % 2)) for t in range(8)]
+    wh = lax.ppermute(w, "tp", swap_pair)
+    swap_both = [
+        (c * 8 + t, (c + 16) % 32 * 8 + u) for c in range(32) for t, u in swap_pair
+    ]
+    wzh = lax.ppermute(w, ("ctx", "tp"), swap_both)
     o4, st = attention(lengths, q4, kvg)
-    return combine_project(o4, st, out_weight, wz)
+    return combine_project(o4, st, out_weight, wz, wh, wzh)
 
 
 def solution(mesh):

time: 142 us -> 144 us (1.014)
  Pallas kernels: 131 us -> 111 us
  waiting for transfers between devices: 0.01 us -> 19.2 us
  local copies, waits for them, and re-layouts: 5.42 us -> 7.31 us
    pallas_call x1, Pallas kernels: 79.7 us -> 59 us  [combine_project(): pl.pallas_call(combine_project_kernel, name='combine_project', out_shape=...]
    ppermute x1 -> x3, waiting for transfers between devices: 0.01 us -> 19.2 us  [the longest x1 19.2 us: body(): wh = lax.ppermute(w, 'tp', swap_pair)]
    ppermute x1 -> x3, starting transfers between devices: 2.47 us -> 3.55 us  [the longest x1 2.47 us: body(): wzh = lax.ppermute(w, ('ctx', 'tp'), swap_both)]
    unnamed x19 -> x15, local copies, waits for them, and re-layouts: 5.33 us -> 6.27 us
  transfers between devices with their start and end apart: 1 -> 3, of which waited for: 0 -> 1; matrix products, arithmetic and copies ran while one was open for 2% -> 0% of each run, Pallas kernels for 36% -> 18%
where the time goes in v3:
time: 144 us
  Pallas kernels  111 us (77%)
  waiting for transfers between devices  19.2 us (13%)
  local copies, waits for them, and re-layouts  7.31 us (5%)
  starting transfers between devices  3.55 us (2%)
  other arithmetic  2.15 us (1%)
    pallas_call x1, Pallas kernels, combine_project(): pl.pallas_call(combine_project_kernel, name='combine_project', out_shape=...  59 us
    pallas_call x1, Pallas kernels, attention(): pl.pallas_call(attention_kernel, name='attention', out_shape=(jax.ShapeDt...  25.9 us
    pallas_call x1, Pallas kernels, gather(): pl.pallas_call(gather_kernel, name='gather_qkv', out_shape=(jax.ShapeDtyp...  25.7 us
    ppermute x1, waiting for transfers between devices, body(): wh = lax.ppermute(w, 'tp', swap_pair)  19.2 us
    unnamed x15, local copies, waits for them, and re-layouts  6.27 us
  transfers between devices with their start and end apart: 3, of which 1 were waited for; matrix products, arithmetic and copies ran while one was open for 0% of the time, Pallas kernels for 18%

profile of v3, /device:TPU:1, one launch (start us, length us, event | category | flops | bytes accessed | tf_op | source)
XLA Modules:
  0.0 143.6 jit_solution(968773988848149827)
XLA Ops:
  0.7 1.0 fusion.11
  1.7 0.3 multiply_cosine_fusion.1
  2.0 0.3 fusion.10
  2.4 1.0 copy.20
  3.4 1.0 convert_bitcast_fusion
  4.4 0.0 copy-start.3
  4.4 0.1 copy.11
  4.5 0.3 subtract_convert_fusion
  4.8 0.1 pad_maximum_fusion
  5.0 0.1 maximum_maximum_fusion.kv_ref
  5.1 25.7 %gather_qkv.1 = (bf16[4,128,1024]{2,1,0:T(8,128)(2,1)S(1)}, bf16[8,640,256]{2,1,0:T(8,128)(2,1)S(1)}) custom-call(bf16[128,1024]{1,0:T(8,128)(2,1)S(1)} %bitcast.26, bf16[640,256]{1,0:T(8,128)(2,1)S(1)} %maximum_maximum_fusion.kv_ref), custom_call_target="tpu_custom_call" | custom-call | tf_op jit(solution)/shard_map/gather_qkv/pallas_call | solution.py:167
  30.7 0.0 copy-start
  30.7 1.5 %copy-done = bf16[8,640,256]{2,1,0:T(8,128)(2,1)} copy-done((bf16[8,640,256]{2,1,0:T(8,128)(2,1)}, bf16[8,640,256]{2,1,0:T(8,128)(2,1)S(1)}, u32[]{:S(2)}) %copy-start) | copy-done | bytes 2621464
  32.2 0.0 copy-start.2
  32.2 1.0 copy-done.2
  33.2 0.0 copy-done.3
  33.2 2.5 %collective-permute-start.2 = (bf16[1024,256]{1,0:T(8,128)(2,1)S(1)}, bf16[1024,256]{1,0:T(8,128)(2,1)S(1)}, u32[]{:S(2)}, u32[]{:S(2)}) collective-permute-start(bf16[1024,256]{1,0:T(8,128)(2,1)S(1)} %copy-done.3), channel_id=1, source_target_pairs={{0,130},{1,131},{2,128},{3,129},{4,134},{5,135},{6,132},{7,133},{8... | collective-permute-start | bytes 1572872 | tf_op jit(solution)/shard_map/ppermute | solution.py:667
  35.7 0.5 collective-permute-start.1
  36.2 0.6 collective-permute-start
  36.8 25.9 %attention.1 = (bf16[4,128,1024]{2,1,0:T(8,128)(2,1)}, f32[4,8,128]{2,1,0:T(8,128)}) custom-call(s32[64]{0:T(128)} %lens_ref.1, bf16[4,128,1024]{2,1,0:T(8,128)(2,1)} %copy-done.2, bf16[8,640,256]{2,1,0:T(8,128)(2,1)} %copy-done), custom_call_target="tpu_custom_call" | custom-call | tf_op jit(solution)/shard_map/attention/pallas_call | solution.py:313
  62.7 0.0 collective-permute-done.2.wzh_ref
  62.7 19.2 %collective-permute-done.1.wh_ref = bf16[1024,256]{1,0:T(8,128)(2,1)S(1)} collective-permute-done((bf16[1024,256]{1,0:T(8,128)(2,1)S(1)}, bf16[1024,256]{1,0:T(8,128)(2,1)S(1)}, u32[]{:S(2)}, u32[]{:S(2)}) %collective-permute-start.1) | collective-permute-done | bytes 524320 | tf_op jit(solution)/shard_map/ppermute | solution.py:663
  81.9 0.0 collective-permute-done.wz_ref
  81.9 0.0 copy-start.1
  81.9 1.2 copy-done.1
  83.2 0.0 copy-start.4
  83.2 0.7 copy-done.4
  83.9 59.0 %combine_project.1 = bf16[512,256]{1,0:T(8,128)(2,1)S(1)} custom-call(bf16[4,128,1024]{2,1,0:T(8,128)(2,1)S(1)} %copy-done.1, f32[4,8,128]{2,1,0:T(8,128)S(1)} %copy-done.4, bf16[1024,256]{1,0:T(8,128)(2,1)S(1)} %copy-done.3, bf16[1024,256]{1,0:T(8,128)(2,1)} %collective-permute-done.wz_ref, bf16[1024,256]{1,0:T(8,128)(2,1)S(1)} %collective-permute-done.1.wh_ref, ...), custom_call_target="tpu_custom_call" | custom-call | tf_op jit(solution)/shard_map/combine_project/pallas_call | solution.py:618
  142.9 0.7 copy.25
  (5 shorter events, 0.1 us)
Async XLA Ops:
  4.4 28.9 %copy-start.3 = (bf16[1024,256]{1,0:T(8,128)(2,1)S(1)}, bf16[1024,256]{1,0:T(8,128)(2,1)}, u32[]{:S(2)}) copy-start(bf16[1024,256]{1,0:T(8,128)(2,1)} %w_ref.1) | copy-start | bytes 1572868
  30.7 1.5 %copy-start = (bf16[8,640,256]{2,1,0:T(8,128)(2,1)}, bf16[8,640,256]{2,1,0:T(8,128)(2,1)S(1)}, u32[]{:S(2)}) copy-start(bf16[8,640,256]{2,1,0:T(8,128)(2,1)S(1)} %get-tuple-element.11.kvg_ref) | copy-start | bytes 7864324
  32.2 1.0 copy-start.2
  33.2 29.5 %collective-permute-start.2 = (bf16[1024,256]{1,0:T(8,128)(2,1)S(1)}, bf16[1024,256]{1,0:T(8,128)(2,1)S(1)}, u32[]{:S(2)}, u32[]{:S(2)}) collective-permute-start(bf16[1024,256]{1,0:T(8,128)(2,1)S(1)} %copy-done.3), channel_id=1, source_target_pairs={{0,130},{1,131},{2,128},{3,129},{4,134},{5,135},{6,132},{7,133},{8... | collective-permute-start | bytes 1572872 | tf_op jit(solution)/shard_map/ppermute | solution.py:667
  35.7 46.2 %collective-permute-start.1 = (bf16[1024,256]{1,0:T(8,128)(2,1)S(1)}, bf16[1024,256]{1,0:T(8,128)(2,1)S(1)}, u32[]{:S(2)}, u32[]{:S(2)}) collective-permute-start(bf16[1024,256]{1,0:T(8,128)(2,1)S(1)} %copy-done.3), channel_id=1, source_target_pairs={{0,2},{1,3},{2,0},{3,1},{4,6},{5,7},{6,4},{7,5},{8,10},{9,11},{10,... | collective-permute-start | bytes 1572872 | tf_op jit(solution)/shard_map/ppermute | solution.py:663
  36.2 45.7 %collective-permute-start = (bf16[1024,256]{1,0:T(8,128)(2,1)S(1)}, bf16[1024,256]{1,0:T(8,128)(2,1)}, u32[]{:S(2)}, u32[]{:S(2)}) collective-permute-start(bf16[1024,256]{1,0:T(8,128)(2,1)S(1)} %copy-done.3), channel_id=1, source_target_pairs={{0,128},{8,136},{16,144},{24,152},{32,160},{40,168},{48,176},{56,1... | collective-permute-start | bytes 1572872 | tf_op jit(solution)/shard_map/ppermute | solution.py:661
  81.9 1.2 copy-start.1
  83.2 0.7 copy-start.4

commit v4 on v0

v4 whole, which is shorter than its diff:
```python
import math

import jax
import jax.numpy as jnp
from jax import lax
from jax.experimental import pallas as pl
from jax.experimental.pallas import tpu as pltpu
from jax.sharding import PartitionSpec as P

SLOT = 256
HD = 128
TOK = 128
HEADS = 8
KV_ROWS = 640
CH = 512
A_ROWS = 256
ROWS = HEADS * TOK
BLK = 512
COLS = 256
HALF = TOK // 2
COPIES = 80
lowest_score = -1e30
rope_base = 500000.0
MESH = pl.DeviceIdType.MESH
SCALE2 = math.log2(math.e) / math.sqrt(HD)


def rotate(values, positions):
    head_size = values.shape[-1]
    half_dim = head_size // 2
    frequency = jnp.exp(
        jnp.arange(half_dim, dtype=jnp.float32) * (-2.0 * math.log(rope_base) / head_size)
    )
    angles = positions.astype(jnp.float32)[:, None] * frequency[None, :]
    cosine = jnp.cos(angles)[:, None, :]
    sine_part = jnp.sin(angles)[:, None, :]
    first_half = values[..., :half_dim]
    second_half = values[..., half_dim:]
    return jnp.concatenate(
        [
            first_half * cosine - second_half * sine_part,
            second_half * cosine + first_half * sine_part,
        ],
        axis=-1,
    )


def coords():
    c = lax.axis_index("ctx")
    z = c // 16
    x = (c // 4) % 4
    y = c % 4
    return z, x, y


def ctx_of(z, x, y):
    return z * 16 + x * 4 + y


def entry_barrier(devices):
    barrier = pltpu.get_barrier_semaphore()
    for d in devices:
        pl.semaphore_signal(barrier, inc=1, device_id=d, device_id_type=MESH)
    pl.semaphore_wait(barrier, len(devices))


def fold(op, values):
    out = values[:, 0:HD]
    for n in range(1, values.shape[1] // HD):
        out = op(out, values[:, n * HD : (n + 1) * HD])
    return out


def wide(values):
    return jnp.concatenate([values] * (CH // HD), axis=1)


def fused_kernel(
    lens_ref,
    q_ref,
    kv_ref,
    w_ref,
    out_ref,
    qh,
    kvg,
    bias,
    sbuf,
    mx,
    top,
    den,
    acc,
    o4,
    st,
    part,
    stat,
    table,
    fwd,
    away,
    wz,
    wh,
    wzh,
    att,
    prod,
    give,
    got,
    keep,
    box,
    ssem,
    rsem,
    core_s,
    core_r,
    z_s,
    z_r,
):
    z, x, y = coords()
    tp = lax.axis_index("tp")
    core = tp % 2
    high = tp // 2
    even = high % 2
    zo = 1 - z
    other = {"tp": tp + 1 - 2 * core}
    pair = {"tp": tp + 2 - 4 * even}
    pos = 2 * high + z
    column = []
    for d in range(1, 8):
        q = (pos + d) % 8
        column.append({"ctx": ctx_of(q % 2, x, y), "tp": (q // 2) * 2 + core})
    xp, xm, x2 = (x + 1) % 4, (x + 3) % 4, (x + 2) % 4
    yp, ym, y2 = (y + 1) % 4, (y + 3) % 4, (y + 2) % 4
    dz = {"ctx": ctx_of(zo, x, y)}
    dxp = {"ctx": ctx_of(z, xp, y)}
    dxm = {"ctx": ctx_of(z, xm, y)}
    dyp = {"ctx": ctx_of(z, x, yp)}
    dym = {"ctx": ctx_of(z, x, ym)}
    dy2 = {"ctx": ctx_of(z, x, y2)}

    table_of = {}

    def view(place):
        if isinstance(place, tuple):
            return place[0].at[place[1:]]
        return place

    def copy(name, src, dst, device):
        n = table_of.setdefault(name, len(table_of))
        return pltpu.make_async_remote_copy(
            src_ref=view(src),
            dst_ref=view(dst),
            send_sem=ssem.at[n],
            recv_sem=rsem.at[n],
            device_id=device,
            device_id_type=MESH,
        )

    makers = {}

    def start(name, src, dst, device):
        def make():
            return copy(name, src, dst, device)

        makers[name] = make
        make().start()

    def wait(*names):
        for name in names:
            makers[name]().wait_recv()

    own = z * 4 + x
    a = pl.ds(0, A_ROWS)
    a0 = pl.ds(0, A_ROWS // 2)
    a1 = pl.ds(A_ROWS // 2, A_ROWS // 2)
    nb = KV_ROWS - A_ROWS
    b = pl.ds(A_ROWS, nb)
    b0 = pl.ds(A_ROWS, nb // 2)
    b1 = pl.ds(A_ROWS + nb // 2, nb // 2)
    h0 = pl.ds(0, ROWS // 2)
    h1 = pl.ds(ROWS // 2, ROWS // 2)

    entry_barrier([dxp, dxm, dyp, dym, dy2, other] + column)

    def kv_send(name, j, rows, device):
        start(name, (kvg, j, rows), (kvg, j, rows), device)

    def kv_own(name, rows, device):
        start(name, (kv_ref, rows), (kvg, own, rows), device)

    kv_own("b_z", b, dz)
    kv_own("b_xp", b, dxp)
    kv_own("b_xm", b, dxm)
    for h in range(HEADS):
        qh[y, h * TOK : (h + 1) * TOK, :] = q_ref[:, h * HD : (h + 1) * HD]
    start("q_yp", (qh, y), (qh, y), dyp)
    start("q_ym", (qh, y), (qh, y), dym)
    kv_own("a_xp", a, dxp)
    kv_own("a_xm", a, dxm)
    kv_own("a_z", a, dz)
    kvg[own] = kv_ref[...]

    lane = lax.broadcasted_iota(jnp.int32, (1, SLOT), 1)
    for j in range(8):
        for s in range(2):
            n = lens_ref[2 * (4 * j + y) + s]
            bias[j : j + 1, s * SLOT : (s + 1) * SLOT] = jnp.where(lane < n, 0.0, lowest_score)
    top[...] = jnp.full(top.shape, lowest_score, jnp.float32)
    den[...] = jnp.zeros_like(den)
    acc[...] = jnp.zeros_like(acc)

    def first(i, j, slot):
        s = lax.dot_general(
            qh[i],
            kvg[j, 0:CH, 0:HD],
            (((1,), (1,)), ((), ())),
            preferred_element_type=jnp.float32,
        )
        s = s + bias[pl.ds(j, 1), :]
        sbuf[slot] = s
        mx[slot] = fold(jnp.maximum, s)

    def span_part(g, lanes):
        return jnp.concatenate([kvg[4 * g + k, CH:KV_ROWS, lanes] for k in range(4)], axis=0)

    def first_span(i, g, slot):
        s = lax.dot_general(
            qh[i],
            span_part(g, slice(0, HD)),
            (((1,), (1,)), ((), ())),
            preferred_element_type=jnp.float32,
        )
        parts = []
        row = lax.broadcasted_iota(jnp.int32, (TOK, TOK), 0)
        col = lax.broadcasted_iota(jnp.int32, (TOK, TOK), 1)
        for k in range(4):
            ahead = (4 * (4 * g + k) + y - 4 * own - i) * TOK
            parts.append(jnp.where(col + ahead <= row, 0.0, lowest_score))
        mask = jnp.concatenate(parts, axis=1)
        s = s + jnp.concatenate([mask] * HEADS, axis=0)
        sbuf[slot] = s
        mx[slot] = fold(jnp.maximum, s)

    def fold_in(i, slot, values):
        old = top[i]
        peak = jnp.max(mx[slot], axis=1, keepdims=True) * SCALE2
        new = jnp.maximum(old, jnp.broadcast_to(peak, (ROWS, HD)))
        factor = jnp.exp2(old - new)
        top[i] = new
        p = jnp.exp2(sbuf[slot] * SCALE2 - wide(new)).astype(jnp.bfloat16)
        both = jnp.dot(
            p,
            jnp.concatenate([values, jnp.ones_like(values)], axis=1),
            preferred_element_type=jnp.float32,
        )
        acc[i] = acc[i] * factor + both[:, 0:HD]
        den[i] = den[i] * factor + both[:, HD : 2 * HD]

    def second(i, j, slot):
        fold_in(i, slot, kvg[j, 0:CH, HD : 2 * HD])

    def second_span(i, g, slot):
        fold_in(i, slot, span_part(g, slice(HD, 2 * HD)))

    first(y, own, 0)

    wait("b_z")
    oz = zo * 4 + x
    own2, far_m, far_p, far_2 = z * 4 + x2, zo * 4 + xm, zo * 4 + xp, zo * 4 + x2
    kv_send("bz_xp", oz, b, dxp)
    kv_send("bz_xm", oz, b, dxm)
    wait("b_xp")
    kv_send("bf_xp", z * 4 + xm, b0, dxp)
    wait("b_xm")
    kv_send("bf_xm", z * 4 + xp, b1, dxm)
    wait("q_yp")
    start("qf_yp", (qh, ym, h0), (qh, ym, h0), dyp)
    wait("q_ym")
    start("qf_ym", (qh, yp, h1), (qh, yp, h1), dym)
    wait("a_xp")
    kv_send("af_xp", z * 4 + xm, a0, dxp)
    kv_send("az_m", z * 4 + xm, a, dz)
    wait("a_xm")
    kv_send("af_xm", z * 4 + xp, a1, dxm)
    kv_send("az_p", z * 4 + xp, a, dz)
    wait("a_z")

    def early(k):
        step = k % 3
        return (z + k // 3) % 2 * 4 + (x + step + step // 2) % 4

    def tile(d):
        return (y + d) % 4

    def pass_queries():
        wait("qf_yp", "qf_ym")

    def pass_b():
        wait("bz_xp")
        kv_send("bzf_xp", far_m, b0, dxp)
        wait("bz_xm")
        kv_send("bzf_xm", far_p, b1, dxm)

    def pass_a():
        wait("af_xp")
        kv_send("az_2a", own2, a0, dz)
        wait("af_xm")
        kv_send("az_2b", own2, a1, dz)

    def start_weights():
        start("w_z", w_ref, wz, dz)
        start("w_h", w_ref, wh, pair)

    points = {2: pass_queries, 3: pass_b, 5: pass_a, 6: start_weights}

    @pl.loop(0, 7)
    def _(step):
        for at, action in points.items():
            pl.when(step == at)(action)
        for u in range(2):
            n = 2 * step + u
            first(tile((n + 1) // 4), early((n + 1) % 4), 1 - u)
            second(tile(n // 4), early(n % 4), u)

    late = (own2, far_p, far_m, far_2)
    first(tile(3), early(3), 1)
    second(tile(3), early(2), 0)
    wait("bf_xp", "bf_xm", "bzf_xp", "bzf_xm", "az_m", "az_p", "az_2a", "az_2b")
    first(tile(1), late[0], 0)
    second(tile(3), early(3), 1)

    lane_t = lax.broadcasted_iota(jnp.int32, (TOK, HD), 1)
    t0 = pl.ds(0, HALF)
    t1 = pl.ds(HALF, HALF)

    def send_yp():
        start("to_p", (o4, 0), (part, 2), dyp)
        start("st_p", (st, 0), (stat, 2), dyp)

    def send_far():
        start("far_p", (o4, 1, t0), (fwd, 0), dyp)
        start("far_m", (o4, 1, t1), (fwd, 1), dym)
        start("st_2", (st, 1), (stat, 1), dy2)

    def send_ym():
        start("to_m", (o4, 2), (part, 0), dym)
        start("st_m", (st, 2), (stat, 0), dym)
        wait("far_p")
        start("fw_p", (fwd, 0), (part, 1, t0), dyp)
        wait("far_m")
        start("fw_m", (fwd, 1), (part, 1, t1), dym)

    @pl.loop(0, 4)
    def _(t):
        i = tile(t + 1)
        for k in range(3):
            first(i, late[k + 1], (k + 1) % 2)
            second(i, late[k], k % 2)
        first_span(i, 0, 0)
        second(i, late[3], 1)
        first_span(i, 1, 1)
        second_span(i, 0, 0)
        first(tile(t + 2), late[0], 0)
        second_span(i, 1, 1)
        total = den[i]
        o = acc[i] / total
        lse = top[i] + jnp.log2(total)
        packed = jnp.zeros((TOK, HD), jnp.float32)
        for h in range(HEADS):
            rows = slice(h * TOK, (h + 1) * TOK)
            o4[t, :, h * HD : (h + 1) * HD] = o[rows].astype(jnp.bfloat16)
            packed = jnp.where(lane_t == h, lse[rows], packed)
        st[t] = packed.T[0:HEADS]
        pl.when(t == 0)(send_yp)
        pl.when(t == 1)(send_far)
        pl.when(t == 2)(send_ym)

    wait("st_p", "st_m", "st_2")
    s_own = st[3]
    s_p, s_m, s_2 = stat[0], stat[2], stat[1]
    best = jnp.maximum(jnp.maximum(s_own, s_p), jnp.maximum(s_m, s_2))
    e_own = jnp.exp2(s_own - best)
    e_p = jnp.exp2(s_p - best)
    e_m = jnp.exp2(s_m - best)
    e_2 = jnp.exp2(s_2 - best)
    norm = 1.0 / (e_own + e_p + e_m + e_2)
    table[...] = jnp.concatenate(
        [e_own * norm, e_p * norm, e_m * norm, e_2 * norm, jnp.zeros((96, TOK), jnp.float32)],
        axis=0,
    ).T
    wait("to_p", "to_m", "fw_p", "fw_m")
    slot_own = x * 4 + y

    def combined(begin, dest):
        rows = pl.ds(pl.multiple_of(begin, HALF), HALF)
        for h in range(HEADS):
            lanes = slice(h * HD, (h + 1) * HD)
            out = o4[3, rows, lanes].astype(jnp.float32) * table[rows, h : h + 1]
            out += part[0, rows, lanes].astype(jnp.float32) * table[rows, 8 + h : 9 + h]
            out += part[2, rows, lanes].astype(jnp.float32) * table[rows, 16 + h : 17 + h]
            out += part[1, rows, lanes].astype(jnp.float32) * table[rows, 24 + h : 25 + h]
            dest[:, lanes] = out.astype(jnp.bfloat16)

    combined((1 - even) * HALF, away)
    start("swap", away, (att, 1, slot_own), pair)
    combined(even * HALF, att.at[0, slot_own])
    lo, hi, full = pl.ds(0, HALF // 2), pl.ds(HALF // 2, HALF // 2), pl.ds(0, HALF)

    def send(name, k, slot, rows, device):
        start(name, (att, k, slot, rows), (att, k, slot, rows), device)

    def both_y(r, xs):
        send("ayp%d" % r, 0, xs * 4 + y, full, dyp)
        send("aym%d" % r, 0, xs * 4 + y, full, dym)

    def both_x(r, ys):
        send("bxp%d" % r, 1, x * 4 + ys, full, dxp)
        send("bxm%d" % r, 1, x * 4 + ys, full, dxm)

    send("axp", 0, slot_own, full, dxp)
    send("axm", 0, slot_own, full, dxm)
    both_y(0, x)
    wait("axp")
    send("axfp", 0, xm * 4 + y, lo, dxp)
    both_y(3, xm)
    wait("axm")
    send("axfm", 0, xp * 4 + y, hi, dxm)
    both_y(1, xp)
    wait("swap")
    send("byp", 1, slot_own, full, dyp)
    send("bym", 1, slot_own, full, dym)
    both_x(0, y)
    wait("w_h")
    start("w_zh", wh, wzh, dz)

    def relay_a(r):
        xs = (x + r) % 4
        wait("ayp%d" % r)
        send("lap%d" % r, 0, xs * 4 + ym, lo, dyp)
        wait("aym%d" % r)
        send("lam%d" % r, 0, xs * 4 + yp, hi, dym)

    def relay_b(r):
        ys = (y + r) % 4
        wait("bxp%d" % r)
        send("lbp%d" % r, 1, xm * 4 + ys, lo, dxp)
        wait("bxm%d" % r)
        send("lbm%d" % r, 1, xp * 4 + ys, hi, dxm)

    def core_copy(n):
        return pltpu.make_async_remote_copy(
            src_ref=give.at[n],
            dst_ref=got.at[n],
            send_sem=core_s.at[n],
            recv_sem=core_r.at[n],
            device_id=other,
            device_id_type=MESH,
        )

    def z_copy(row, n, far):
        return pltpu.make_async_remote_copy(
            src_ref=keep.at[n, far],
            dst_ref=box.at[high],
            send_sem=z_s.at[2 * n + far],
            recv_sem=z_r.at[high],
            device_id={
                "ctx": ctx_of(zo if far else z, x, y),
                "tp": (2 * z + row // 2) * 2 + core,
            },
            device_id_type=MESH,
        )

    def product(row, n):
        keeps = row % 2 == core
        slots = pl.ds(4 * row, 4)
        rows_a = att[0, slots].reshape(BLK // 2, HEADS * HD)
        rows_b = att[1, slots].reshape(BLK // 2, HEADS * HD)
        for far, (wa, wb) in enumerate(((w_ref, wh), (wz, wzh))):
            prod[n % 2, far] = jnp.dot(
                rows_a, wa[...], preferred_element_type=jnp.float32
            ) + jnp.dot(rows_b, wb[...], preferred_element_type=jnp.float32)

        @pl.when(jnp.logical_not(keeps))
        def _():
            give[n] = prod[n % 2].astype(jnp.bfloat16)
            core_copy(n).start()

    def settle(row, n):
        keeps = row % 2 == core
        remote = 2 * z + row // 2 != high

        @pl.when(keeps)
        def _():
            core_copy(n).wait_recv()
            keep[n] = (prod[n % 2] + got[n].astype(jnp.float32)).astype(jnp.bfloat16)
            z_copy(row, n, 1).start()

            @pl.when(remote)
            def _():
                z_copy(row, n, 0).start()

            @pl.when(jnp.logical_not(remote))
            def _():
                box[high] = keep[n, 0]

    relay_a(0)
    wait("byp")
    send("byfp", 1, x * 4 + ym, lo, dyp)
    both_x(3, ym)
    wait("bym")
    send("byfm", 1, x * 4 + yp, hi, dym)
    both_x(1, yp)
    wait("axfp", "axfm")
    both_y(2, x2)
    relay_a(3)
    relay_b(0)
    wait("byfp", "byfm")
    both_x(2, y2)
    wait("lap0", "lam0", "w_z", "w_zh")
    product(x, 0)
    relay_a(1)
    settle(x, 0)
    relay_b(3)
    relay_b(1)
    relay_a(2)
    relay_b(2)
    wait("lap3", "lam3")
    product(xm, 1)
    settle(xm, 1)
    wait("lap1", "lam1")
    product(xp, 2)
    settle(xp, 2)
    wait("lap2", "lam2")
    for r in range(4):
        wait("lbp%d" % r, "lbm%d" % r)
    product(x2, 3)
    settle(x2, 3)

    source_z = high // 2
    for s in range(4):
        arrives = jnp.logical_or(high != s, z != source_z)

        @pl.when(arrives)
        def _(s=s):
            pltpu.make_async_remote_copy(
                src_ref=keep.at[0, 0],
                dst_ref=box.at[s],
                send_sem=z_s.at[0],
                recv_sem=z_r.at[s],
                device_id=other,
                device_id_type=MESH,
            ).wait_recv()

    for e in range(2):
        total = box[e].astype(jnp.float32) + box[2 + e].astype(jnp.float32)
        total = total.astype(jnp.bfloat16)
        for g in range(4):
            begin = g * TOK + e * HALF
            out_ref[begin : begin + HALF] = total[g * HALF : (g + 1) * HALF]
    for n, row in enumerate((x, xm, xp, x2)):
        keeps = row % 2 == core
        remote = 2 * z + row // 2 != high

        @pl.when(keeps)
        def _(n=n, row=row, remote=remote):
            z_copy(row, n, 1).wait_send()

            @pl.when(remote)
            def _():
                z_copy(row, n, 0).wait_send()

        @pl.when(jnp.logical_not(keeps))
        def _(n=n):
            core_copy(n).wait_send()

    for make in makers.values():
        make().wait_send()


def fused(lengths, q, kv, w):
    bf16, f32 = jnp.bfloat16, jnp.float32
    return pl.pallas_call(
        fused_kernel,
        name="attention_block",
        out_shape=jax.ShapeDtypeStruct((BLK, COLS), bf16),
        in_specs=[pl.BlockSpec(memory_space=pltpu.SMEM)]
        + [pl.BlockSpec(memory_space=pltpu.VMEM)] * 3,
        out_specs=pl.BlockSpec(memory_space=pltpu.VMEM),
        scratch_shapes=[
            pltpu.VMEM((4, ROWS, HD), bf16),
            pltpu.VMEM((8, KV_ROWS, 2 * HD), bf16),
            pltpu.VMEM((8, CH), f32),
            pltpu.VMEM((2, ROWS, CH), f32),
            pltpu.VMEM((2, ROWS, HD), f32),
            pltpu.VMEM((4, ROWS, HD), f32),
            pltpu.VMEM((4, ROWS, HD), f32),
            pltpu.VMEM((4, ROWS, HD), f32),
            pltpu.VMEM((4, TOK, HEADS * HD), bf16),
            pltpu.VMEM((4, HEADS, TOK), f32),
            pltpu.VMEM((3, TOK, HEADS * HD), bf16),
            pltpu.VMEM((3, HEADS, TOK), f32),
            pltpu.VMEM((TOK, TOK), f32),
            pltpu.VMEM((2, HALF, HEADS * HD), bf16),
            pltpu.VMEM((HALF, HEADS * HD), bf16),
            pltpu.VMEM((HEADS * HD, COLS), bf16),
            pltpu.VMEM((HEADS * HD, COLS), bf16),
            pltpu.VMEM((HEADS * HD, COLS), bf16),
            pltpu.VMEM((2, 16, HALF, HEADS * HD), bf16),
            pltpu.VMEM((2, 2, BLK // 2, COLS), f32),
            pltpu.VMEM((4, 2, BLK // 2, COLS), bf16),
            pltpu.VMEM((4, 2, BLK // 2, COLS), bf16),
            pltpu.VMEM((4, 2, BLK // 2, COLS), bf16),
            pltpu.VMEM((4, BLK // 2, COLS), bf16),
            pltpu.SemaphoreType.DMA((COPIES,)),
            pltpu.SemaphoreType.DMA((COPIES,)),
            pltpu.SemaphoreType.DMA((4,)),
            pltpu.SemaphoreType.DMA((4,)),
            pltpu.SemaphoreType.DMA((8,)),
            pltpu.SemaphoreType.DMA((4,)),
        ],
        compiler_params=pltpu.CompilerParams(
            collective_id=0, has_side_effects=True, vmem_limit_bytes=48 << 20
        ),
    )(lengths, q, kv, w)


def body(queries, span_kv, cache_kv, out_weight, offset, lengths):
    first_token = lax.axis_index("ctx") * TOK
    positions = offset[0] + first_token + jnp.arange(TOK, dtype=jnp.int32)
    rotated = rotate(queries.reshape(TOK, HEADS, HD).astype(jnp.float32), positions)
    rotated = rotated.astype(jnp.bfloat16).reshape(TOK, HEADS * HD)
    keys = rotate(span_kv[:, :, 0, :].astype(jnp.float32), positions).astype(jnp.bfloat16)
    span = jnp.concatenate([keys[:, 0, :], span_kv[:, 0, 1, :]], axis=1)
    kv = jnp.concatenate([cache_kv.reshape(CH, 2 * HD), span], axis=0)
    return fused(lengths, rotated, kv, out_weight)


def solution(mesh):
    return jax.shard_map(
        body,
        mesh=mesh,
        in_specs=(
            P("ctx", "tp"),
            P("ctx", "tp", None, None),
            P("ctx", "tp", None, None),
            P("tp", "ctx"),
            P(),
            P(),
        ),
        out_specs=P("tp", "ctx"),
        check_vma=False,
    )
```

time: 691 us -> 109 us (0.16)
  waiting for transfers between devices: 509 us -> 0 us
  matrix products: 101 us -> 0 us
  Pallas kernels: 0 us -> 101 us
  other arithmetic: 29.7 us -> 2.15 us
  local copies, waits for them, and re-layouts: 28 us -> 3.25 us
  between operations: 14 us -> 0.78 us
  loops' own time: 7.33 us -> 0 us
    all_gather x3 -> x0, waiting for transfers between devices: 448 us -> none  [the longest x1 173 us: body(): lax.all_gather(attention, 'ctx', axis=0, tiled=True)]
    dot_general x21 -> x0, matrix products: 101 us -> none  [the longest x10 47.4 us: online_update(): jnp.einsum('tkgd,nkd->tkgn', grouped, key_rows, preferred_element_type=jn...]
    pallas_call x0 -> x1, Pallas kernels: none -> 101 us  [fused(): pl.pallas_call(fused_kernel, name='attention_block', out_shape=jax.ShapeD...]
    reduce_scatter x1 -> x0, waiting for transfers between devices: 61.6 us -> none  [body(): lax.psum_scatter(projected.astype(jnp.bfloat16), 'tp', scatter_dimension=...]
    reduce_sum x18 -> x0, other arithmetic: 26.6 us -> none  [the longest x10 25.3 us: online_update(): running_sum = running_sum * factor + jnp.sum(weights, axis=-1)]
    slice x4 -> x0, local copies, waits for them, and re-layouts: 11.3 us -> none  [the longest x3 9.72 us: fold_blocks(): piece[:, :, 1, :].reshape(block_count, block, kv_local, head_size)]
    another operation x2 -> x0, loops' own time: 7.33 us -> none  [fold_blocks(): lax.scan(advance, carry_state, (key_rows, value_rows, jnp.arange(block_co...]
  transfers between devices with their start and end apart: 4 -> 0, of which waited for: 4 -> 0; matrix products, arithmetic and copies ran while one was open for 1% -> 0% of each run, Pallas kernels for 0% -> 0%
where the time goes in v4:
time: 109 us; the launch traced here: 107 us
  Pallas kernels  101 us (93%)
  local copies, waits for them, and re-layouts  3.25 us (3%)
  other arithmetic  2.15 us (2%)
    pallas_call x1, Pallas kernels, fused(): pl.pallas_call(fused_kernel, name='attention_block', out_shape=jax.ShapeD...  101 us
    unnamed x13, local copies, waits for them, and re-layouts  3.16 us

profile of v4, /device:TPU:1, one launch (start us, length us, event | category | flops | bytes accessed | tf_op | source)
XLA Modules:
  0.0 107.0 jit_solution(12907933240848986764)
XLA Ops:
  0.7 0.3 multiply_cosine_fusion.1
  1.0 1.0 convert_bitcast_fusion
  2.0 0.1 copy.11
  2.1 0.3 subtract_convert_fusion
  2.4 0.1 pad_maximum_fusion
  2.5 0.0 copy-start.3
  2.6 0.8 copy-done.3
  3.4 0.1 fusion.11
  3.5 0.0 copy-start.2
  3.5 0.3 fusion.10
  3.8 0.6 copy-done.2
  4.4 0.0 copy-start
  4.5 0.0 copy-start.1
  4.5 0.1 maximum_maximum_fusion.kv_ref
  4.6 0.9 copy-done
  5.5 0.0 copy-done.1
  5.5 100.8 %attention_block.1 = bf16[512,256]{1,0:T(8,128)(2,1)S(1)} custom-call(s32[64]{0:T(128)S(1)} %copy-done.1, bf16[128,1024]{1,0:T(8,128)(2,1)S(1)} %bitcast.26, bf16[640,256]{1,0:T(8,128)(2,1)S(1)} %maximum_maximum_fusion.kv_ref, bf16[1024,256]{1,0:T(8,128)(2,1)S(1)} %copy-done), custom_call_target="tpu_custom_call" | custom-call | tf_op jit(solution)/shard_map/attention_block/pallas_call | solution.py:578
  106.3 0.7 copy.25
  (6 shorter events, 0.1 us)
Async XLA Ops:
  2.5 0.8 copy-start.3
  3.5 1.0 copy-start.2
  4.4 1.0 copy-start
  4.5 1.0 copy-start.1

commit v5 on v4

--- a/solution.py
+++ b/solution.py
@@ -18,6 +18,7 @@
 BLK = 512
 COLS = 256
 HALF = TOK // 2
+WP = 128
 COPIES = 80
 lowest_score = -1e30
 rope_base = 500000.0
@@ -107,6 +108,8 @@
     box,
     ssem,
     rsem,
+    w_s,
+    w_r,
     core_s,
     core_r,
     z_s,
@@ -260,26 +263,18 @@
 
     first(y, own, 0)
 
-    wait("b_z")
     oz = zo * 4 + x
     own2, far_m, far_p, far_2 = z * 4 + x2, zo * 4 + xm, zo * 4 + xp, zo * 4 + x2
+    own_m, own_p = z * 4 + xm, z * 4 + xp
+    wait("b_z", "b_xp", "b_xm", "a_xp", "a_xm", "a_z")
     kv_send("bz_xp", oz, b, dxp)
     kv_send("bz_xm", oz, b, dxm)
-    wait("b_xp")
-    kv_send("bf_xp", z * 4 + xm, b0, dxp)
-    wait("b_xm")
-    kv_send("bf_xm", z * 4 + xp, b1, dxm)
-    wait("q_yp")
-    start("qf_yp", (qh, ym, h0), (qh, ym, h0), dyp)
-    wait("q_ym")
-    start("qf_ym", (qh, yp, h1), (qh, yp, h1), dym)
-    wait("a_xp")
-    kv_send("af_xp", z * 4 + xm, a0, dxp)
-    kv_send("az_m", z * 4 + xm, a, dz)
-    wait("a_xm")
-    kv_send("af_xm", z * 4 + xp, a1, dxm)
-    kv_send("az_p", z * 4 + xp, a, dz)
-    wait("a_z")
+    kv_send("az_m", own_m, a, dz)
+    kv_send("az_p", own_p, a, dz)
+    kv_send("bf_xp", own_m, b0, dxp)
+    kv_send("bf_xm", own_p, b1, dxm)
+    kv_send("af_xp", own_m, a0, dxp)
+    kv_send("af_xm", own_p, a1, dxm)
 
     def early(k):
         step = k % 3
@@ -289,6 +284,12 @@
         return (y + d) % 4
 
     def pass_queries():
+        wait("q_yp")
+        start("qf_yp", (qh, ym, h0), (qh, ym, h0), dyp)
+        wait("q_ym")
+        start("qf_ym", (qh, yp, h1), (qh, yp, h1), dym)
+
+    def wait_queries():
         wait("qf_yp", "qf_ym")
 
     def pass_b():
@@ -303,11 +304,7 @@
         wait("af_xm")
         kv_send("az_2b", own2, a1, dz)
 
-    def start_weights():
-        start("w_z", w_ref, wz, dz)
-        start("w_h", w_ref, wh, pair)
-
-    points = {2: pass_queries, 3: pass_b, 5: pass_a, 6: start_weights}
+    points = {0: pass_queries, 3: wait_queries, 4: pass_b, 5: pass_a}
 
     @pl.loop(0, 7)
     def _(step):
@@ -325,6 +322,34 @@
     first(tile(1), late[0], 0)
     second(tile(3), early(3), 1)
 
+    def piece(kind, c):
+        src, dst, device = ((w_ref, wh, pair), (w_ref, wz, dz), (wh, wzh, dz))[kind]
+        rows = pl.ds(pl.multiple_of(c * WP, WP), WP)
+        return pltpu.make_async_remote_copy(
+            src_ref=src.at[rows],
+            dst_ref=dst.at[rows],
+            send_sem=w_s.at[kind, c],
+            recv_sem=w_r.at[kind, c],
+            device_id=device,
+            device_id_type=MESH,
+        )
+
+    def send_piece(n):
+        c = n % 8
+
+        @pl.when(n // 8 == 0)
+        def _():
+            piece(0, c).start()
+
+        @pl.when(n // 8 == 1)
+        def _():
+            piece(1, c).start()
+
+        @pl.when(n // 8 == 2)
+        def _():
+            piece(0, c).wait_recv()
+            piece(2, c).start()
+
     lane_t = lax.broadcasted_iota(jnp.int32, (TOK, HD), 1)
     t0 = pl.ds(0, HALF)
     t1 = pl.ds(HALF, HALF)
@@ -350,12 +375,16 @@
     def _(t):
         i = tile(t + 1)
         for k in range(3):
+            send_piece(6 * t + k)
             first(i, late[k + 1], (k + 1) % 2)
             second(i, late[k], k % 2)
+        send_piece(6 * t + 3)
         first_span(i, 0, 0)
         second(i, late[3], 1)
+        send_piece(6 * t + 4)
         first_span(i, 1, 1)
         second_span(i, 0, 0)
+        send_piece(6 * t + 5)
         first(tile(t + 2), late[0], 0)
         second_span(i, 1, 1)
         total = den[i]
@@ -426,8 +455,6 @@
     send("byp", 1, slot_own, full, dyp)
     send("bym", 1, slot_own, full, dym)
     both_x(0, y)
-    wait("w_h")
-    start("w_zh", wh, wzh, dz)
 
     def relay_a(r):
         xs = (x + r) % 4
@@ -512,7 +539,10 @@
     relay_b(0)
     wait("byfp", "byfm")
     both_x(2, y2)
-    wait("lap0", "lam0", "w_z", "w_zh")
+    wait("lap0", "lam0")
+    for c in range(8):
+        piece(1, c).wait_recv()
+        piece(2, c).wait_recv()
     product(x, 0)
     relay_a(1)
     settle(x, 0)
@@ -571,6 +601,9 @@
 
     for make in makers.values():
         make().wait_send()
+    for kind in range(3):
+        for c in range(8):
+            piece(kind, c).wait_send()
 
 
 def fused(lengths, q, kv, w):
@@ -609,6 +642,8 @@
             pltpu.VMEM((4, BLK // 2, COLS), bf16),
             pltpu.SemaphoreType.DMA((COPIES,)),
             pltpu.SemaphoreType.DMA((COPIES,)),
+            pltpu.SemaphoreType.DMA((3, 8)),
+            pltpu.SemaphoreType.DMA((3, 8)),
             pltpu.SemaphoreType.DMA((4,)),
             pltpu.SemaphoreType.DMA((4,)),
             pltpu.SemaphoreType.DMA((8,)),

time: 109 us -> 107 us (0.982); the launches traced: 107 us -> 106 us
  no operation moved by 1% of the time
where the time goes in v5:
time: 107 us; the launch traced here: 106 us
  Pallas kernels  100 us (93%)
  local copies, waits for them, and re-layouts  3.25 us (3%)
  other arithmetic  2.15 us (2%)
    pallas_call x1, Pallas kernels, fused(): pl.pallas_call(fused_kernel, name='attention_block', out_shape=jax.ShapeD...  100 us
    unnamed x13, local copies, waits for them, and re-layouts  3.16 us

profile of v5, /device:TPU:1, one launch (start us, length us, event | category | flops | bytes accessed | tf_op | source)
XLA Modules:
  0.0 106.3 jit_solution(3335171205074733564)
XLA Ops:
  0.7 0.3 multiply_cosine_fusion.1
  1.0 1.0 convert_bitcast_fusion
  2.0 0.1 copy.11
  2.1 0.3 subtract_convert_fusion
  2.4 0.1 pad_maximum_fusion
  2.5 0.0 copy-start.3
  2.6 0.8 copy-done.3
  3.4 0.1 fusion.11
  3.5 0.0 copy-start.2
  3.5 0.3 fusion.10
  3.8 0.6 copy-done.2
  4.4 0.0 copy-start
  4.5 0.0 copy-start.1
  4.5 0.1 maximum_maximum_fusion.kv_ref
  4.6 0.9 copy-done
  5.5 0.0 copy-done.1
  5.5 100.2 %attention_block.1 = bf16[512,256]{1,0:T(8,128)(2,1)S(1)} custom-call(s32[64]{0:T(128)S(1)} %copy-done.1, bf16[128,1024]{1,0:T(8,128)(2,1)S(1)} %bitcast.26, bf16[640,256]{1,0:T(8,128)(2,1)S(1)} %maximum_maximum_fusion.kv_ref, bf16[1024,256]{1,0:T(8,128)(2,1)S(1)} %copy-done), custom_call_target="tpu_custom_call" | custom-call | tf_op jit(solution)/shard_map/attention_block/pallas_call | solution.py:611
  105.6 0.7 copy.25
  (6 shorter events, 0.1 us)
Async XLA Ops:
  2.5 0.8 copy-start.3
  3.5 1.0 copy-start.2
  4.4 1.0 copy-start
  4.5 1.0 copy-start.1

commit v6 on v4

--- a/solution.py
+++ b/solution.py
@@ -18,31 +18,22 @@
 BLK = 512
 COLS = 256
 HALF = TOK // 2
-COPIES = 80
+WP = 256
+COPIES = 72
 lowest_score = -1e30
 rope_base = 500000.0
 MESH = pl.DeviceIdType.MESH
 SCALE2 = math.log2(math.e) / math.sqrt(HD)
 
 
-def rotate(values, positions):
-    head_size = values.shape[-1]
-    half_dim = head_size // 2
+def rotary_tables(positions):
+    half = HD // 2
     frequency = jnp.exp(
-        jnp.arange(half_dim, dtype=jnp.float32) * (-2.0 * math.log(rope_base) / head_size)
+        jnp.arange(half, dtype=jnp.float32) * (-2.0 * math.log(rope_base) / HD)
     )
     angles = positions.astype(jnp.float32)[:, None] * frequency[None, :]
-    cosine = jnp.cos(angles)[:, None, :]
-    sine_part = jnp.sin(angles)[:, None, :]
-    first_half = values[..., :half_dim]
-    second_half = values[..., half_dim:]
-    return jnp.concatenate(
-        [
-            first_half * cosine - second_half * sine_part,
-            second_half * cosine + first_half * sine_part,
-        ],
-        axis=-1,
-    )
+    cosine, sine = jnp.cos(angles), jnp.sin(angles)
+    return jnp.concatenate([cosine, cosine], axis=1), jnp.concatenate([-sine, sine], axis=1)
 
 
 def coords():
@@ -78,9 +69,13 @@
 def fused_kernel(
     lens_ref,
     q_ref,
-    kv_ref,
+    cache_ref,
+    span_ref,
+    cos_ref,
+    sin_ref,
+    w_hbm,
+    out_ref,
     w_ref,
-    out_ref,
     qh,
     kvg,
     bias,
@@ -107,6 +102,10 @@
     box,
     ssem,
     rsem,
+    w_s,
+    w_r,
+    w_local,
+    near,
     core_s,
     core_r,
     z_s,
@@ -176,25 +175,44 @@
     h0 = pl.ds(0, ROWS // 2)
     h1 = pl.ds(ROWS // 2, ROWS // 2)
 
-    entry_barrier([dxp, dxm, dyp, dym, dy2, other] + column)
+    next_z, last_z = column[0], column[6]
+    entry_barrier([dxp, dxm, dyp, dym, other, next_z, last_z])
+
+    def near_signal(r):
+        for device in (next_z, last_z):
+            pl.semaphore_signal(near.at[r], inc=1, device_id=device, device_id_type=MESH)
+
+    def near_wait(r):
+        pl.semaphore_wait(near.at[r], 2)
+
+    near_signal(0)
 
     def kv_send(name, j, rows, device):
         start(name, (kvg, j, rows), (kvg, j, rows), device)
 
+    def rotated(values):
+        values = values.astype(jnp.float32)
+        turned = jnp.concatenate([values[:, HD // 2 :], values[:, : HD // 2]], axis=1)
+        return (values * cos_ref[...] + turned * sin_ref[...]).astype(jnp.bfloat16)
+
     def kv_own(name, rows, device):
-        start(name, (kv_ref, rows), (kvg, own, rows), device)
-
+        kv_send(name, own, rows, device)
+
+    kvg[own, 0:CH] = cache_ref[...]
+    kvg[own, CH:KV_ROWS, 0:HD] = rotated(span_ref[:, 0:HD])
+    kvg[own, CH:KV_ROWS, HD : 2 * HD] = span_ref[:, HD : 2 * HD]
     kv_own("b_z", b, dz)
     kv_own("b_xp", b, dxp)
     kv_own("b_xm", b, dxm)
     for h in range(HEADS):
-        qh[y, h * TOK : (h + 1) * TOK, :] = q_ref[:, h * HD : (h + 1) * HD]
+        qh[y, h * TOK : (h + 1) * TOK, :] = rotated(q_ref[:, h * HD : (h + 1) * HD])
     start("q_yp", (qh, y), (qh, y), dyp)
     start("q_ym", (qh, y), (qh, y), dym)
     kv_own("a_xp", a, dxp)
     kv_own("a_xm", a, dxm)
     kv_own("a_z", a, dz)
-    kvg[own] = kv_ref[...]
+    weights_here = pltpu.make_async_copy(w_hbm, w_ref, w_local)
+    weights_here.start()
 
     lane = lax.broadcasted_iota(jnp.int32, (1, SLOT), 1)
     for j in range(8):
@@ -260,27 +278,9 @@
 
     first(y, own, 0)
 
-    wait("b_z")
     oz = zo * 4 + x
     own2, far_m, far_p, far_2 = z * 4 + x2, zo * 4 + xm, zo * 4 + xp, zo * 4 + x2
-    kv_send("bz_xp", oz, b, dxp)
-    kv_send("bz_xm", oz, b, dxm)
-    wait("b_xp")
-    kv_send("bf_xp", z * 4 + xm, b0, dxp)
-    wait("b_xm")
-    kv_send("bf_xm", z * 4 + xp, b1, dxm)
-    wait("q_yp")
-    start("qf_yp", (qh, ym, h0), (qh, ym, h0), dyp)
-    wait("q_ym")
-    start("qf_ym", (qh, yp, h1), (qh, yp, h1), dym)
-    wait("a_xp")
-    kv_send("af_xp", z * 4 + xm, a0, dxp)
-    kv_send("az_m", z * 4 + xm, a, dz)
-    wait("a_xm")
-    kv_send("af_xm", z * 4 + xp, a1, dxm)
-    kv_send("az_p", z * 4 + xp, a, dz)
-    wait("a_z")
-
+    own_m, own_p = z * 4 + xm, z * 4 + xp
     def early(k):
         step = k % 3
         return (z + k // 3) % 2 * 4 + (x + step + step // 2) % 4
@@ -288,14 +288,52 @@
     def tile(d):
         return (y + d) % 4
 
-    def pass_queries():
+    def early_tile(n):
+        k = n % 4
+        return tile(k + k // 2 - 2 * (k // 3))
+
+    def piece(kind, c):
+        src, dst, device = ((w_hbm, wh, pair), (w_hbm, wz, dz), (wh, wzh, dz))[kind]
+        rows = pl.ds(c * WP, WP)
+        return pltpu.make_async_remote_copy(
+            src_ref=src.at[rows],
+            dst_ref=dst.at[rows],
+            send_sem=w_s.at[kind, c],
+            recv_sem=w_r.at[kind, c],
+            device_id=device,
+            device_id_type=MESH,
+        )
+
+    def pass_first():
+        wait("b_z", "b_xp", "b_xm", "a_xp", "a_xm", "a_z")
+        kv_send("bz_xp", oz, b, dxp)
+        kv_send("bz_xm", oz, b, dxm)
+        kv_send("az_m", own_m, a, dz)
+        kv_send("az_p", own_p, a, dz)
+        kv_send("bf_xp", own_m, b0, dxp)
+        kv_send("bf_xm", own_p, b1, dxm)
+        kv_send("af_xp", own_m, a0, dxp)
+        kv_send("af_xm", own_p, a1, dxm)
         wait("qf_yp", "qf_ym")
+
+    def pass_weights(c):
+        def action():
+            if c == 0:
+                near_wait(0)
+                near_signal(1)
+            piece(0, c).start()
+            if c == 2:
+                near_wait(1)
+                near_signal(2)
+
+        return action
 
     def pass_b():
         wait("bz_xp")
         kv_send("bzf_xp", far_m, b0, dxp)
         wait("bz_xm")
         kv_send("bzf_xm", far_p, b1, dxm)
+        pass_weights(3)()
 
     def pass_a():
         wait("af_xp")
@@ -303,11 +341,21 @@
         wait("af_xm")
         kv_send("az_2b", own2, a1, dz)
 
-    def start_weights():
-        start("w_z", w_ref, wz, dz)
-        start("w_h", w_ref, wh, pair)
-
-    points = {2: pass_queries, 3: pass_b, 5: pass_a, 6: start_weights}
+    oz = zo * 4 + x
+    own2, far_m, far_p, far_2 = z * 4 + x2, zo * 4 + xm, zo * 4 + xp, zo * 4 + x2
+    own_m, own_p = z * 4 + xm, z * 4 + xp
+    wait("q_yp")
+    start("qf_yp", (qh, ym, h0), (qh, ym, h0), dyp)
+    wait("q_ym")
+    start("qf_ym", (qh, yp, h1), (qh, yp, h1), dym)
+    points = {
+        1: pass_first,
+        2: pass_weights(0),
+        3: pass_weights(1),
+        4: pass_weights(2),
+        5: pass_b,
+        6: pass_a,
+    }
 
     @pl.loop(0, 7)
     def _(step):
@@ -315,15 +363,33 @@
             pl.when(step == at)(action)
         for u in range(2):
             n = 2 * step + u
-            first(tile((n + 1) // 4), early((n + 1) % 4), 1 - u)
-            second(tile(n // 4), early(n % 4), u)
+            first(early_tile(n + 1), early((n + 1) // 4), 1 - u)
+            second(early_tile(n), early(n // 4), u)
 
     late = (own2, far_p, far_m, far_2)
-    first(tile(3), early(3), 1)
-    second(tile(3), early(2), 0)
-    wait("bf_xp", "bf_xm", "bzf_xp", "bzf_xm", "az_m", "az_p", "az_2a", "az_2b")
+    first(tile(2), early(3), 1)
+    second(tile(3), early(3), 0)
+    wait("bf_xp", "bf_xm", "az_m", "az_p")
     first(tile(1), late[0], 0)
-    second(tile(3), early(3), 1)
+    second(tile(2), early(3), 1)
+
+    def wait_last():
+        wait("bzf_xp", "bzf_xm", "az_2a", "az_2b")
+        near_wait(2)
+
+    def send_piece(t, k):
+        if k < 4:
+
+            @pl.when(t == 0)
+            def _():
+                piece(1, k).start()
+
+        if k > 1:
+
+            @pl.when(t == 3)
+            def _():
+                piece(0, k - 2).wait_recv()
+                piece(2, k - 2).start()
 
     lane_t = lax.broadcasted_iota(jnp.int32, (TOK, HD), 1)
     t0 = pl.ds(0, HALF)
@@ -350,12 +416,18 @@
     def _(t):
         i = tile(t + 1)
         for k in range(3):
+            send_piece(t, k)
+            if k == 2:
+                pl.when(t == 0)(wait_last)
             first(i, late[k + 1], (k + 1) % 2)
             second(i, late[k], k % 2)
+        send_piece(t, 3)
         first_span(i, 0, 0)
         second(i, late[3], 1)
+        send_piece(t, 4)
         first_span(i, 1, 1)
         second_span(i, 0, 0)
+        send_piece(t, 5)
         first(tile(t + 2), late[0], 0)
         second_span(i, 1, 1)
         total = den[i]
@@ -397,8 +469,6 @@
             out += part[1, rows, lanes].astype(jnp.float32) * table[rows, 24 + h : 25 + h]
             dest[:, lanes] = out.astype(jnp.bfloat16)
 
-    combined((1 - even) * HALF, away)
-    start("swap", away, (att, 1, slot_own), pair)
     combined(even * HALF, att.at[0, slot_own])
     lo, hi, full = pl.ds(0, HALF // 2), pl.ds(HALF // 2, HALF // 2), pl.ds(0, HALF)
 
@@ -416,6 +486,8 @@
     send("axp", 0, slot_own, full, dxp)
     send("axm", 0, slot_own, full, dxm)
     both_y(0, x)
+    combined((1 - even) * HALF, away)
+    start("swap", away, (att, 1, slot_own), pair)
     wait("axp")
     send("axfp", 0, xm * 4 + y, lo, dxp)
     both_y(3, xm)
@@ -426,8 +498,6 @@
     send("byp", 1, slot_own, full, dyp)
     send("bym", 1, slot_own, full, dym)
     both_x(0, y)
-    wait("w_h")
-    start("w_zh", wh, wzh, dz)
 
     def relay_a(r):
         xs = (x + r) % 4
@@ -512,7 +582,11 @@
     relay_b(0)
     wait("byfp", "byfm")
     both_x(2, y2)
-    wait("lap0", "lam0", "w_z", "w_zh")
+    wait("lap0", "lam0")
+    for c in range(4):
+        piece(1, c).wait_recv()
+        piece(2, c).wait_recv()
+    weights_here.wait()
     product(x, 0)
     relay_a(1)
     settle(x, 0)
@@ -571,18 +645,23 @@
 
     for make in makers.values():
         make().wait_send()
-
-
-def fused(lengths, q, kv, w):
+    for kind in range(3):
+        for c in range(4):
+            piece(kind, c).wait_send()
+
+
+def fused(lengths, q, cache, span, cosine, sine, w):
     bf16, f32 = jnp.bfloat16, jnp.float32
     return pl.pallas_call(
         fused_kernel,
         name="attention_block",
         out_shape=jax.ShapeDtypeStruct((BLK, COLS), bf16),
         in_specs=[pl.BlockSpec(memory_space=pltpu.SMEM)]
-        + [pl.BlockSpec(memory_space=pltpu.VMEM)] * 3,
+        + [pl.BlockSpec(memory_space=pltpu.VMEM)] * 5
+        + [pl.BlockSpec(memory_space=pltpu.HBM)],
         out_specs=pl.BlockSpec(memory_space=pltpu.VMEM),
         scratch_shapes=[
+            pltpu.VMEM((HEADS * HD, COLS), bf16),
             pltpu.VMEM((4, ROWS, HD), bf16),
             pltpu.VMEM((8, KV_ROWS, 2 * HD), bf16),
             pltpu.VMEM((8, CH), f32),
@@ -609,6 +688,10 @@
             pltpu.VMEM((4, BLK // 2, COLS), bf16),
             pltpu.SemaphoreType.DMA((COPIES,)),
             pltpu.SemaphoreType.DMA((COPIES,)),
+            pltpu.SemaphoreType.DMA((3, 4)),
+            pltpu.SemaphoreType.DMA((3, 4)),
+            pltpu.SemaphoreType.DMA,
+            pltpu.SemaphoreType.REGULAR((3,)),
             pltpu.SemaphoreType.DMA((4,)),
             pltpu.SemaphoreType.DMA((4,)),
             pltpu.SemaphoreType.DMA((8,)),
@@ -617,18 +700,16 @@
         compiler_params=pltpu.CompilerParams(
             collective_id=0, has_side_effects=True, vmem_limit_bytes=48 << 20
         ),
-    )(lengths, q, kv, w)
+    )(lengths, q, cache, span, cosine, sine, w)
 
 
 def body(queries, span_kv, cache_kv, out_weight, offset, lengths):
     first_token = lax.axis_index("ctx") * TOK
     positions = offset[0] + first_token + jnp.arange(TOK, dtype=jnp.int32)
-    rotated = rotate(queries.reshape(TOK, HEADS, HD).astype(jnp.float32), positions)
-    rotated = rotated.astype(jnp.bfloat16).reshape(TOK, HEADS * HD)
-    keys = rotate(span_kv[:, :, 0, :].astype(jnp.float32), positions).astype(jnp.bfloat16)
-    span = jnp.concatenate([keys[:, 0, :], span_kv[:, 0, 1, :]], axis=1)
-    kv = jnp.concatenate([cache_kv.reshape(CH, 2 * HD), span], axis=0)
-    return fused(lengths, rotated, kv, out_weight)
+    cosine, sine = rotary_tables(positions)
+    cache = cache_kv.reshape(CH, 2 * HD)
+    span = span_kv.reshape(TOK, 2 * HD)
+    return fused(lengths, queries, cache, span, cosine, sine, out_weight)
 
 
 def solution(mesh):

time: 109 us -> 108 us (level); the launches traced: 107 us -> 108 us
  Pallas kernels: 101 us -> 104 us
  other arithmetic: 2.15 us -> 0.42 us
    pallas_call x1, Pallas kernels: 101 us -> 104 us  [fused(): pl.pallas_call(fused_kernel, name='attention_block', out_shape=jax.ShapeD...]
    unnamed x13 -> x11, local copies, waits for them, and re-layouts: 3.16 us -> 3.05 us
where the time goes in v6:
time: 108 us
  Pallas kernels  104 us (96%)
  local copies, waits for them, and re-layouts  3.05 us (3%)
    pallas_call x1, Pallas kernels, fused(): pl.pallas_call(fused_kernel, name='attention_block', out_shape=jax.ShapeD...  104 us
    unnamed x11, local copies, waits for them, and re-layouts  3.05 us

profile of v6, /device:TPU:1, one launch (start us, length us, event | category | flops | bytes accessed | tf_op | source)
XLA Modules:
  0.0 108.1 jit_solution(6273502373772149393)
XLA Ops:
  0.7 0.9 copy.12
  1.5 0.0 copy-start.3
  1.5 0.0 copy-start
  1.6 0.3 fusion
  1.9 0.1 pad_maximum_fusion
  2.0 0.5 copy-done.3
  2.5 0.0 copy-start.1
  2.5 0.0 copy-start.2
  2.5 0.1 copy-done
  2.7 0.8 copy-done.1
  3.5 0.0 copy-done.2
  3.5 103.9 %attention_block.1 = bf16[512,256]{1,0:T(8,128)(2,1)S(1)} custom-call(s32[64]{0:T(128)S(1)} %copy-done.2, bf16[128,1024]{1,0:T(8,128)(2,1)S(1)} %copy-done.1, bf16[512,256]{1,0:T(8,128)(2,1)S(1)} %bitcast.12, bf16[128,256]{1,0:T(8,128)(2,1)S(1)} %bitcast.13, f32[128,128]{1,0:T(8,128)S(1)} %get-tuple-element.8.cos_ref, ...), custom_call_target="tpu_custom_call" | custom-call | tf_op jit(solution)/shard_map/attention_block/pallas_call | solution.py:655
  107.4 0.7 copy.15
  (3 shorter events, 0.1 us)
Async XLA Ops:
  1.5 1.0 copy-start.3
  1.5 1.1 %copy-start = (bf16[1024,256]{1,0:T(8,128)(2,1)S(1)}, bf16[1024,256]{1,0:T(8,128)(2,1)}, u32[]{:S(2)}) copy-start(bf16[1024,256]{1,0:T(8,128)(2,1)} %w_hbm.1) | copy-start | bytes 1572868
  2.5 1.0 copy-start.1
  2.5 0.9 copy-start.2

commit v7 on v6

--- a/solution.py
+++ b/solution.py
@@ -316,24 +316,19 @@
         kv_send("af_xm", own_p, a1, dxm)
         wait("qf_yp", "qf_ym")
 
-    def pass_weights(c):
-        def action():
-            if c == 0:
-                near_wait(0)
-                near_signal(1)
-            piece(0, c).start()
-            if c == 2:
-                near_wait(1)
-                near_signal(2)
-
-        return action
+    def round_one():
+        near_wait(0)
+        near_signal(1)
+
+    def round_two():
+        near_wait(1)
+        near_signal(2)
 
     def pass_b():
         wait("bz_xp")
         kv_send("bzf_xp", far_m, b0, dxp)
         wait("bz_xm")
         kv_send("bzf_xm", far_p, b1, dxm)
-        pass_weights(3)()
 
     def pass_a():
         wait("af_xp")
@@ -350,9 +345,8 @@
     start("qf_ym", (qh, yp, h1), (qh, yp, h1), dym)
     points = {
         1: pass_first,
-        2: pass_weights(0),
-        3: pass_weights(1),
-        4: pass_weights(2),
+        2: round_one,
+        4: round_two,
         5: pass_b,
         6: pass_a,
     }
@@ -377,19 +371,28 @@
         wait("bzf_xp", "bzf_xm", "az_2a", "az_2b")
         near_wait(2)
 
+    def forward_piece(c):
+        piece(0, c).wait_recv()
+        piece(2, c).start()
+
+    pieces = {
+        (0, 0): lambda: piece(0, 0).start(),
+        (0, 1): lambda: piece(0, 1).start(),
+        (0, 2): lambda: piece(1, 0).start(),
+        (0, 3): lambda: piece(0, 2).start(),
+        (0, 4): lambda: piece(0, 3).start(),
+        (0, 5): lambda: piece(1, 1).start(),
+        (1, 2): lambda: piece(1, 2).start(),
+        (1, 4): lambda: piece(1, 3).start(),
+        (2, 2): lambda: forward_piece(0),
+        (2, 5): lambda: forward_piece(1),
+        (3, 5): lambda: forward_piece(2),
+    }
+
     def send_piece(t, k):
-        if k < 4:
-
-            @pl.when(t == 0)
-            def _():
-                piece(1, k).start()
-
-        if k > 1:
-
-            @pl.when(t == 3)
-            def _():
-                piece(0, k - 2).wait_recv()
-                piece(2, k - 2).start()
+        for (at, item), action in pieces.items():
+            if item == k:
+                pl.when(t == at)(action)
 
     lane_t = lax.broadcasted_iota(jnp.int32, (TOK, HD), 1)
     t0 = pl.ds(0, HALF)
@@ -495,6 +498,7 @@
     send("axfm", 0, xp * 4 + y, hi, dxm)
     both_y(1, xp)
     wait("swap")
+    forward_piece(3)
     send("byp", 1, slot_own, full, dyp)
     send("bym", 1, slot_own, full, dym)
     both_x(0, y)
@@ -536,20 +540,27 @@
             device_id_type=MESH,
         )
 
-    def product(row, n):
-        keeps = row % 2 == core
+    def half_product(row, n, far):
+        wa, wb = (wz, wzh) if far else (w_ref, wh)
         slots = pl.ds(4 * row, 4)
         rows_a = att[0, slots].reshape(BLK // 2, HEADS * HD)
         rows_b = att[1, slots].reshape(BLK // 2, HEADS * HD)
-        for far, (wa, wb) in enumerate(((w_ref, wh), (wz, wzh))):
-            prod[n % 2, far] = jnp.dot(
-                rows_a, wa[...], preferred_element_type=jnp.float32
-            ) + jnp.dot(rows_b, wb[...], preferred_element_type=jnp.float32)
+        prod[n % 2, far] = jnp.dot(rows_a, wa[...], preferred_element_type=jnp.float32) + jnp.dot(
+            rows_b, wb[...], preferred_element_type=jnp.float32
+        )
+
+    def hand_over(row, n):
+        keeps = row % 2 == core
 
         @pl.when(jnp.logical_not(keeps))
         def _():
             give[n] = prod[n % 2].astype(jnp.bfloat16)
             core_copy(n).start()
+
+    def product(row, n):
+        half_product(row, n, 0)
+        half_product(row, n, 1)
+        hand_over(row, n)
 
     def settle(row, n):
         keeps = row % 2 == core
@@ -583,17 +594,19 @@
     wait("byfp", "byfm")
     both_x(2, y2)
     wait("lap0", "lam0")
+    weights_here.wait()
+    half_product(x, 0, 0)
+    relay_a(1)
+    relay_b(3)
+    relay_b(1)
     for c in range(4):
         piece(1, c).wait_recv()
         piece(2, c).wait_recv()
-    weights_here.wait()
-    product(x, 0)
-    relay_a(1)
-    settle(x, 0)
-    relay_b(3)
-    relay_b(1)
+    half_product(x, 0, 1)
+    hand_over(x, 0)
     relay_a(2)
     relay_b(2)
+    settle(x, 0)
     wait("lap3", "lam3")
     product(xm, 1)
     settle(xm, 1)

time: 108 us -> 108 us (level)
  no operation moved by 1% of the time
where the time goes in v7:
time: 108 us
  Pallas kernels  104 us (96%)
  local copies, waits for them, and re-layouts  3.05 us (3%)
    pallas_call x1, Pallas kernels, fused(): pl.pallas_call(fused_kernel, name='attention_block', out_shape=jax.ShapeD...  104 us
    unnamed x11, local copies, waits for them, and re-layouts  3.05 us

profile of v7, /device:TPU:1, one launch (start us, length us, event | category | flops | bytes accessed | tf_op | source)
XLA Modules:
  0.0 108.1 jit_solution(9441325566827247527)
XLA Ops:
  0.7 0.9 copy.12
  1.5 0.0 copy-start.3
  1.5 0.0 copy-start
  1.6 0.3 fusion
  1.9 0.1 pad_maximum_fusion
  2.0 0.5 copy-done.3
  2.5 0.0 copy-start.1
  2.5 0.0 copy-start.2
  2.5 0.1 copy-done
  2.7 0.8 copy-done.1
  3.5 0.0 copy-done.2
  3.5 103.9 %attention_block.1 = bf16[512,256]{1,0:T(8,128)(2,1)S(1)} custom-call(s32[64]{0:T(128)S(1)} %copy-done.2, bf16[128,1024]{1,0:T(8,128)(2,1)S(1)} %copy-done.1, bf16[512,256]{1,0:T(8,128)(2,1)S(1)} %bitcast.12, bf16[128,256]{1,0:T(8,128)(2,1)S(1)} %bitcast.13, f32[128,128]{1,0:T(8,128)S(1)} %get-tuple-element.8.cos_ref, ...), custom_call_target="tpu_custom_call" | custom-call | tf_op jit(solution)/shard_map/attention_block/pallas_call | solution.py:668
  107.4 0.7 copy.15
  (3 shorter events, 0.1 us)
Async XLA Ops:
  1.5 1.0 copy-start.3
  1.5 1.1 %copy-start = (bf16[1024,256]{1,0:T(8,128)(2,1)S(1)}, bf16[1024,256]{1,0:T(8,128)(2,1)}, u32[]{:S(2)}) copy-start(bf16[1024,256]{1,0:T(8,128)(2,1)} %w_hbm.1) | copy-start | bytes 1572868
  2.5 1.0 copy-start.1
  2.5 0.9 copy-start.2

commit v8 on v7

--- a/solution.py
+++ b/solution.py
@@ -18,7 +18,7 @@
 BLK = 512
 COLS = 256
 HALF = TOK // 2
-WP = 256
+WP = 128
 COPIES = 72
 lowest_score = -1e30
 rope_base = 500000.0
@@ -294,7 +294,7 @@
 
     def piece(kind, c):
         src, dst, device = ((w_hbm, wh, pair), (w_hbm, wz, dz), (wh, wzh, dz))[kind]
-        rows = pl.ds(c * WP, WP)
+        rows = pl.ds(pl.multiple_of(c * WP, WP), WP)
         return pltpu.make_async_remote_copy(
             src_ref=src.at[rows],
             dst_ref=dst.at[rows],
@@ -371,28 +371,22 @@
         wait("bzf_xp", "bzf_xm", "az_2a", "az_2b")
         near_wait(2)
 
-    def forward_piece(c):
-        piece(0, c).wait_recv()
-        piece(2, c).start()
-
-    pieces = {
-        (0, 0): lambda: piece(0, 0).start(),
-        (0, 1): lambda: piece(0, 1).start(),
-        (0, 2): lambda: piece(1, 0).start(),
-        (0, 3): lambda: piece(0, 2).start(),
-        (0, 4): lambda: piece(0, 3).start(),
-        (0, 5): lambda: piece(1, 1).start(),
-        (1, 2): lambda: piece(1, 2).start(),
-        (1, 4): lambda: piece(1, 3).start(),
-        (2, 2): lambda: forward_piece(0),
-        (2, 5): lambda: forward_piece(1),
-        (3, 5): lambda: forward_piece(2),
-    }
-
     def send_piece(t, k):
-        for (at, item), action in pieces.items():
-            if item == k:
-                pl.when(t == at)(action)
+        n = 6 * t + k
+        c = n % 8
+
+        @pl.when(n // 8 == 0)
+        def _():
+            piece(0, c).start()
+
+        @pl.when(n // 8 == 1)
+        def _():
+            piece(1, c).start()
+
+        @pl.when(n // 8 == 2)
+        def _():
+            piece(0, c).wait_recv()
+            piece(2, c).start()
 
     lane_t = lax.broadcasted_iota(jnp.int32, (TOK, HD), 1)
     t0 = pl.ds(0, HALF)
@@ -498,7 +492,6 @@
     send("axfm", 0, xp * 4 + y, hi, dxm)
     both_y(1, xp)
     wait("swap")
-    forward_piece(3)
     send("byp", 1, slot_own, full, dyp)
     send("bym", 1, slot_own, full, dym)
     both_x(0, y)
@@ -596,17 +589,17 @@
     wait("lap0", "lam0")
     weights_here.wait()
     half_product(x, 0, 0)
-    relay_a(1)
-    relay_b(3)
-    relay_b(1)
-    for c in range(4):
+    for c in range(8):
         piece(1, c).wait_recv()
         piece(2, c).wait_recv()
     half_product(x, 0, 1)
     hand_over(x, 0)
+    relay_a(1)
+    settle(x, 0)
+    relay_b(3)
+    relay_b(1)
     relay_a(2)
     relay_b(2)
-    settle(x, 0)
     wait("lap3", "lam3")
     product(xm, 1)
     settle(xm, 1)
@@ -659,7 +652,7 @@
     for make in makers.values():
         make().wait_send()
     for kind in range(3):
-        for c in range(4):
+        for c in range(8):
             piece(kind, c).wait_send()
 
 
@@ -701,8 +694,8 @@
             pltpu.VMEM((4, BLK // 2, COLS), bf16),
             pltpu.SemaphoreType.DMA((COPIES,)),
             pltpu.SemaphoreType.DMA((COPIES,)),
-            pltpu.SemaphoreType.DMA((3, 4)),
-            pltpu.SemaphoreType.DMA((3, 4)),
+            pltpu.SemaphoreType.DMA((3, 8)),
+            pltpu.SemaphoreType.DMA((3, 8)),
             pltpu.SemaphoreType.DMA,
             pltpu.SemaphoreType.REGULAR((3,)),
             pltpu.SemaphoreType.DMA((4,)),

time: 108 us -> 106 us (0.981)
  Pallas kernels: 104 us -> 101 us
    pallas_call x1, Pallas kernels: 104 us -> 101 us  [fused(): pl.pallas_call(fused_kernel, name='attention_block', out_shape=jax.ShapeD...]
where the time goes in v8:
time: 106 us; the launch traced here: 105 us
  Pallas kernels  101 us (95%)
  local copies, waits for them, and re-layouts  3.05 us (3%)
    pallas_call x1, Pallas kernels, fused(): pl.pallas_call(fused_kernel, name='attention_block', out_shape=jax.ShapeD...  101 us
    unnamed x11, local copies, waits for them, and re-layouts  3.05 us

profile of v8, /device:TPU:1, one launch (start us, length us, event | category | flops | bytes accessed | tf_op | source)
XLA Modules:
  0.0 105.2 jit_solution(13385735850351812241)
XLA Ops:
  0.7 0.9 copy.12
  1.5 0.0 copy-start.3
  1.5 0.0 copy-start
  1.6 0.3 fusion
  1.9 0.1 pad_maximum_fusion
  2.0 0.5 copy-done.3
  2.5 0.0 copy-start.1
  2.5 0.0 copy-start.2
  2.5 0.1 copy-done
  2.7 0.8 copy-done.1
  3.5 0.0 copy-done.2
  3.5 101.0 %attention_block.1 = bf16[512,256]{1,0:T(8,128)(2,1)S(1)} custom-call(s32[64]{0:T(128)S(1)} %copy-done.2, bf16[128,1024]{1,0:T(8,128)(2,1)S(1)} %copy-done.1, bf16[512,256]{1,0:T(8,128)(2,1)S(1)} %bitcast.12, bf16[128,256]{1,0:T(8,128)(2,1)S(1)} %bitcast.13, f32[128,128]{1,0:T(8,128)S(1)} %get-tuple-element.8.cos_ref, ...), custom_call_target="tpu_custom_call" | custom-call | tf_op jit(solution)/shard_map/attention_block/pallas_call | solution.py:661
  104.5 0.7 copy.15
  (3 shorter events, 0.1 us)
Async XLA Ops:
  1.5 1.0 copy-start.3
  1.5 1.1 %copy-start = (bf16[1024,256]{1,0:T(8,128)(2,1)S(1)}, bf16[1024,256]{1,0:T(8,128)(2,1)}, u32[]{:S(2)}) copy-start(bf16[1024,256]{1,0:T(8,128)(2,1)} %w_hbm.1) | copy-start | bytes 1572868
  2.5 1.0 copy-start.1
  2.5 0.9 copy-start.2
